TPU v7x, 128 devices: a whole 4x4x4 slice. The times are simulated.
128 devices in a mesh: grp: 4 (over x), dom: 32 (over y, z, core).
Axes of the slice: x: 4, y: 4, z: 4, core: 2. Of those that a mesh axis runs over, the one named last changes fastest.
Arguments:
- forcing: float32 [3, 8192, 512], P(None, 'dom'), may hold values from -144 to 144
- viscosity: float32 [8192], P('dom'), may hold values from 0.3 to 3
- mass_coef: float32 [8192], P('dom'), may hold values from 8 to 80
- element_order: int32 [32, 256], P('dom'), may hold values from 0 to 255, each once within a row
- owner: int32 [32, 256], P('dom'), may hold values from -1 to 31, as said below
Outputs:
- fields: float32 [4, 8192, 512], P('grp', 'dom')
Inputs may be any that keep to these rules, and one draw needn't show every extreme that they name: `element_order`: row d gives each element slot of partition d its cell in the partition's brick of 8 x 8 x 4 elements, every cell once. -1 marks an element that is not analysed; at most 8 elements of one partition have the same owner, and some owner gets exactly 8 from every partition.
All inputs are finite; a program needn't handle non-finite values.
Results may differ from a plain program's by a relative error of at most 0.00037.
Values may be sent and summed in bfloat16 or wider, within the bound.
A program may use at most 64 MiB of HBM per device.

v0:
```python
import functools

import jax
import jax.numpy as jnp
import ml_dtypes
import numpy as np
from jax import lax
from jax.experimental import pallas as pl
from jax.experimental.pallas import tpu as pltpu
from jax.sharding import PartitionSpec as P

NP = 8
ITERS = 4
SWEEPS = 4
LAYER = 64
CELLS = 256
NODES = 512
DOMS = 32
BASIS_LOW = 0.3
BASIS_HIGH = 2.0
THETA = 0.5 * (BASIS_LOW + BASIS_HIGH)
DELTA = 0.5 * (BASIS_HIGH - BASIS_LOW)
MESH = pl.DeviceIdType.MESH
F32 = jnp.float32
BF16 = jnp.bfloat16


def legendre_values(points, node_count):
    legendre = np.zeros((points.shape[0], node_count))
    legendre[:, 0] = 1.0
    legendre[:, 1] = points
    for poly_order in range(2, node_count):
        legendre[:, poly_order] = (
            (2 * poly_order - 1) * points * legendre[:, poly_order - 1]
            - (poly_order - 1) * legendre[:, poly_order - 2]
        ) / poly_order
    return legendre


def lobatto_table(node_count):
    degree = node_count - 1
    points = np.cos(np.pi * np.arange(node_count) / degree)
    for attempt in range(60):
        legendre = legendre_values(points, node_count)
        points = points - (points * legendre[:, degree] - legendre[:, degree - 1]) / (
            node_count * legendre[:, degree]
        )
    points = points[::-1].copy()
    end_values = legendre_values(points, node_count)[:, degree]
    weights = 2.0 / (degree * node_count * end_values * end_values)
    spacing = points[:, None] - points[None, :] + np.eye(node_count)
    diff_matrix = end_values[:, None] / end_values[None, :] / spacing
    diff_matrix = diff_matrix * (1.0 - np.eye(node_count))
    diff_matrix[0, 0] = -degree * node_count / 4.0
    diff_matrix[-1, -1] = degree * node_count / 4.0
    return (weights, diff_matrix)


def split_rows(matrix):
    high = matrix.astype(np.float32).astype(ml_dtypes.bfloat16)
    low = (matrix - high.astype(np.float64)).astype(np.float32).astype(ml_dtypes.bfloat16)
    return high, low


def tables():
    weights, diff = lobatto_table(NP)
    eye = np.eye(NP)
    cube = (
        weights[:, None, None] * weights[None, :, None] * weights[None, None, :]
    ).reshape(-1)
    directional = [
        np.kron(eye, np.kron(eye, diff)),
        np.kron(eye, np.kron(diff, eye)),
        np.kron(diff, np.kron(eye, eye)),
    ]
    stiff = np.zeros((NODES, NODES))
    for matrix in directional:
        stiff = stiff + matrix.T @ (cube[:, None] * matrix)
    mats = np.stack([np.stack(split_rows(m)) for m in (stiff, directional[2].T)])
    flat = np.concatenate([directional[0].T[:128, :128], directional[1].T[:128, :128]], 1)
    high, low = split_rows(flat)
    flat = np.concatenate([high, high, low], 0)
    lanes = np.zeros((8, NODES), np.float32)
    lanes[0] = cube
    lanes[1] = np.diag(stiff)
    lanes[2] = np.repeat(diff[NP - 1], LAYER)
    lanes[3] = np.repeat(diff[0], LAYER)
    return mats, flat, lanes


def rotated(value, shift, axis):
    return pltpu.roll(value, shift % value.shape[axis], axis)


def kernel(
    forcing, par_in, owner_in, lanes, flat, mats,
    out,
    fsc, weights, par, parn, pone, ptr, visc, mass, raw, tmp, inv, lhs, v0, v1, v2, v3,
    xs, xlhs, gx, gy, gz, gpack, fbuf, fsend, frecv, moments, red, packed, recv, lam, lamrecv,
    wsem, fsem, psend, precv, gsend, grecv, f3send, f3recv, rsend, rrecv, asend, arecv,
    osend, orecv,
):
    grp = lax.axis_index("grp")
    dom = lax.axis_index("dom")
    comp = jnp.minimum(grp, 2)
    up = lax.rem(dom + 1, DOMS)
    down = lax.rem(dom + DOMS - 1, DOMS)
    barrier = pltpu.get_barrier_semaphore()

    for step in range(1, DOMS):
        pl.semaphore_signal(
            barrier, inc=1, device_id=(grp, lax.rem(dom + step, DOMS)), device_id_type=MESH
        )
    for step in range(1, 4):
        pl.semaphore_signal(
            barrier, inc=1, device_id=(lax.rem(grp + step, 4), dom), device_id_type=MESH
        )

    load_force = pltpu.make_async_copy(forcing.at[comp], fsc, fsem)
    load_force.start()
    load_mats = []
    for which in range(2):
        for part, source in enumerate((0, 0, 1)):
            copy = pltpu.make_async_copy(
                mats.at[which, source],
                weights.at[which, part * NODES : (part + 1) * NODES],
                wsem.at[3 * which + part],
            )
            copy.start()
            load_mats.append(copy)

    lane = lax.broadcasted_iota(jnp.int32, (8, 8, 128), 2)
    sub = lax.broadcasted_iota(jnp.int32, (8, 8, 128), 1)
    node_i = lax.rem(lane, 8)
    node_j = lax.rem(lane // 8, 8)
    x_high = (node_i == 7) & (sub < 7)
    x_low = (node_i == 0) & (sub > 0)
    y_high = node_j == 7
    y_low = node_j == 0
    half_low = lane < LAYER
    has_up = jnp.where(dom < DOMS - 1, 1.0, 0.0).astype(F32)
    has_down = jnp.where(dom > 0, 1.0, 0.0).astype(F32)

    def x_neighbours(a):
        above = rotated(rotated(a, 7, 2), -1, 1)
        below = rotated(rotated(a, -7, 2), 1, 1)
        return jnp.where(x_high, above, jnp.where(x_low, below, 0.0))

    def y_neighbours(a):
        blank = jnp.zeros((1, 8, 128), F32)
        above = jnp.concatenate([rotated(a, 56, 2)[1:], blank], 0)
        below = jnp.concatenate([blank, rotated(a, -56, 2)[:-1]], 0)
        return jnp.where(y_high, above, jnp.where(y_low, below, 0.0))

    def xy_sum(a):
        a = a + x_neighbours(a)
        return a + y_neighbours(a)

    def rows_of(layer):
        return pl.ds(pl.multiple_of(layer * LAYER, LAYER), LAYER)

    def load(ref, layer, tile):
        return ref[rows_of(layer), tile * 128 : tile * 128 + 128].reshape(8, 8, 128)

    def store(ref, layer, tile, value):
        ref[rows_of(layer), tile * 128 : tile * 128 + 128] = value.reshape(LAYER, 128)

    def column(ref, layer):
        return ref[rows_of(layer), :].reshape(8, 8, 128)

    def table(row, tile):
        return lanes[row : row + 1, tile * 128 : tile * 128 + 128].reshape(1, 1, 128)

    def split3(value):
        high = value.astype(BF16)
        rest = value - high.astype(F32)
        middle = rest.astype(BF16)
        low = (rest - middle.astype(F32)).astype(BF16)
        return high, middle, low

    def store_lhs(ref, layer, tile, value):
        value = value.reshape(LAYER, 128)
        high = value.astype(BF16)
        low = (value - high.astype(F32)).astype(BF16)
        ref[rows_of(layer), tile * 128 : tile * 128 + 128] = high
        ref[rows_of(layer), NODES + tile * 128 : NODES + tile * 128 + 128] = low
        ref[rows_of(layer), 2 * NODES + tile * 128 : 2 * NODES + tile * 128 + 128] = high

    cell_sub = lax.broadcasted_iota(jnp.int32, (CELLS, CELLS), 0).astype(F32)
    cell_lane = lax.broadcasted_iota(jnp.int32, (CELLS, CELLS), 1).astype(F32)
    par[...] = par_in[...]

    def coefficients(ref, base, scale):
        hit = ref[2:3, :] == cell_sub
        for row, target in ((0, visc), (1, mass)):
            col = jnp.sum(jnp.where(hit, ref[row : row + 1, :], 0.0), axis=1, keepdims=True)
            target[base : base + CELLS, :] = jnp.broadcast_to(col * scale, (CELLS, 128))
        return hit

    hit = coefficients(par, CELLS, 1.0)
    pone[...] = jnp.where(hit, 1.0, 0.0).astype(BF16)
    order_col = jnp.sum(
        jnp.where(cell_sub == cell_lane, par[2:3, :], 0.0), axis=1, keepdims=True
    )
    ptr[...] = jnp.where(order_col == cell_lane, 1.0, 0.0).astype(BF16)

    load_force.wait()

    def gather_own(tile, carry):
        cols = pl.ds(pl.multiple_of(tile * 128, 128), 128)
        parts = split3(fsc[:, cols])
        total = jnp.zeros((CELLS, 128), F32)
        for part in parts:
            total = total + jnp.dot(pone[...], part, preferred_element_type=F32)
        raw[CELLS : 2 * CELLS, cols] = total * lanes[0:1, cols]
        return carry

    lax.fori_loop(0, 4, gather_own, 0)

    pl.semaphore_wait(barrier, DOMS - 1 + 3)

    def remote(src, dst, send, recv_sem, device):
        return pltpu.make_async_remote_copy(
            src_ref=src, dst_ref=dst, send_sem=send, recv_sem=recv_sem,
            device_id=device, device_id_type=MESH,
        )

    par_copies = [
        remote(par, parn.at[0], psend.at[0], precv.at[0], (grp, up)),
        remote(par, parn.at[1], psend.at[1], precv.at[1], (grp, down)),
    ]
    ghost_copies = [
        remote(
            raw.at[5 * LAYER : 8 * LAYER], raw.at[1 * LAYER : 4 * LAYER],
            gsend.at[0], grecv.at[0], (grp, up),
        ),
        remote(
            raw.at[4 * LAYER : 7 * LAYER], raw.at[8 * LAYER : 11 * LAYER],
            gsend.at[1], grecv.at[1], (grp, down),
        ),
        remote(
            raw.at[4 * LAYER : 5 * LAYER, 384:512], raw.at[0:LAYER, 384:512],
            gsend.at[2], grecv.at[2], (grp, up),
        ),
        remote(
            raw.at[7 * LAYER : 8 * LAYER, 0:128], raw.at[11 * LAYER : 12 * LAYER, 0:128],
            gsend.at[3], grecv.at[3], (grp, down),
        ),
    ]
    for copy in par_copies + ghost_copies:
        copy.start()

    def assemble_xy(layer, tiles, scale):
        coef_v = column(visc, layer)
        coef_m = column(mass, layer)
        for tile in tiles:
            force = load(raw, layer, tile)
            if scale is not None:
                force = force * scale
            store(tmp, layer, tile, xy_sum(force))
            diag = coef_v * table(1, tile) + coef_m * table(0, tile)
            store(inv, layer, tile, xy_sum(diag))

    def over(low, high, body):
        lax.fori_loop(low, high, lambda layer, carry: (body(layer), carry)[1], 0)

    every = (0, 1, 2, 3)
    over(4, 8, lambda layer: assemble_xy(layer, every, None))

    owner_row = owner_in[...].astype(F32)
    owner_col = jnp.sum(
        jnp.where(cell_sub == cell_lane, owner_row, 0.0), axis=1, keepdims=True
    )
    same = (owner_col == owner_row) & (cell_sub < cell_lane)
    rank_row = jnp.sum(jnp.where(same, 1.0, 0.0), axis=0, keepdims=True)
    dest_row = jnp.where(owner_row >= 0.0, owner_row * 8.0 + rank_row, -1.0)
    slot_of = jnp.where(dest_row == cell_sub, 1.0, 0.0).astype(BF16)
    gpack[...] = jnp.dot(slot_of, ptr[...], preferred_element_type=F32).astype(BF16)

    for copy in par_copies:
        copy.wait()
    coefficients(parn.at[0], 0, has_down)
    coefficients(parn.at[1], 2 * CELLS, has_up)
    for copy in ghost_copies:
        copy.wait()

    assemble_xy(0, (3,), has_down)
    over(1, 4, lambda layer: assemble_xy(layer, every, has_down))
    over(8, 11, lambda layer: assemble_xy(layer, every, has_up))
    assemble_xy(11, (0,), has_up)

    def z_sum(ref, layer, tile):
        value = load(ref, layer, tile)
        if tile == 0:
            value = value + jnp.where(half_low, rotated(load(ref, layer - 1, 3), 64, 2), 0.0)
        if tile == 3:
            value = value + jnp.where(half_low, 0.0, rotated(load(ref, layer + 1, 0), 64, 2))
        return value

    def assemble_z(layer):
        for tile in every:
            diag = z_sum(inv, layer, tile)
            force = z_sum(tmp, layer, tile)
            inverse = jnp.where(diag > 0.0, 1.0 / jnp.where(diag > 0.0, diag, 1.0), 0.0)
            store(v1, layer, tile, inverse)
            value = force * inverse
            store(v0, layer, tile, value)
            store_lhs(lhs, layer, tile, value)

    over(1, 11, assemble_z)

    def copy_inverse(layer):
        for tile in every:
            store(inv, layer, tile, load(v1, layer, tile) * (1.0 / DELTA))

    over(2, 10, copy_inverse)

    for copy in load_mats:
        copy.wait()

    def multiply(left, low, high, which, target, target_low):
        def body(half, carry):
            cols = pl.ds(pl.multiple_of(half * 256, 256), 256)
            target[target_low * LAYER : (target_low + high - low) * LAYER, cols] = jnp.dot(
                left[low * LAYER : high * LAYER, :],
                weights[which, :, cols],
                preferred_element_type=F32,
            )
            return carry

        lax.fori_loop(0, 2, body, 0)

    def apply_xy(vec, layer, sums):
        coef_v = column(visc, layer)
        coef_m = column(mass, layer)
        for tile in every:
            value = load(vec, layer, tile)
            image = coef_v * load(tmp, layer, tile) + coef_m * (table(0, tile) * value)
            if sums is not None:
                diag = coef_v * table(1, tile) + coef_m * table(0, tile)
                sums = (
                    sums[0] + jnp.sum(value * image, axis=0),
                    sums[1] + jnp.sum(value * value * diag, axis=0),
                )
            store(tmp, layer, tile, xy_sum(image))
        return sums

    def last_sums(vec, layer, sums):
        coef_v = column(visc, layer)
        coef_m = column(mass, layer)
        for tile in every:
            value = load(vec, layer, tile)
            image = coef_v * load(tmp, layer, tile) + coef_m * (table(0, tile) * value)
            diag = coef_v * table(1, tile) + coef_m * table(0, tile)
            sums = (
                sums[0] + jnp.sum(value * image, axis=0),
                sums[1] + jnp.sum(value * value * diag, axis=0),
            )
        return sums

    def advance(layer, current, previous, following):
        for tile in every:
            value = z_sum(tmp, layer, tile) * load(inv, layer, tile)
            value = value - (THETA / DELTA) * load(current, layer, tile)
            if previous is not None:
                value = 2.0 * value - load(previous, layer, tile)
            store(following, layer, tile, value)
            store_lhs(lhs, layer, tile, value)

    blank = (jnp.zeros((8, 128), F32), jnp.zeros((8, 128), F32))
    basis = (v0, v1, v2, v3)
    for step in range(ITERS):
        low, high = 1 + step, 11 - step
        multiply(lhs, low, high, 0, tmp, low)
        if step + 1 < ITERS:
            over(low, 4, lambda layer: apply_xy(basis[step], layer, None))
            sums = lax.fori_loop(
                4, 8, lambda layer, carry: apply_xy(basis[step], layer, carry), blank
            )
            over(8, high, lambda layer: apply_xy(basis[step], layer, None))
        else:
            sums = lax.fori_loop(
                4, 8, lambda layer, carry: last_sums(basis[step], layer, carry), blank
            )
        moments[step : step + 1, :] = jnp.sum(sums[0], axis=0, keepdims=True)
        moments[4 + step : 5 + step, :] = jnp.sum(sums[1], axis=0, keepdims=True)
        if step + 1 < ITERS:
            over(
                low + 1,
                high - 1,
                lambda layer: advance(
                    layer, basis[step], basis[step - 1] if step else None, basis[step + 1]
                ),
            )

    red[0] = moments[...]
    sum_copies = []
    for step in range(1, DOMS):
        copy = remote(
            moments, red.at[step], rsend, rrecv, (grp, lax.rem(dom + step, DOMS))
        )
        copy.start()

    def end_face(ref, layer, row):
        total = load(ref, layer, 0) * table(row, 0)
        for tile in (1, 2, 3):
            total = total + load(ref, layer, tile) * table(row, tile)
        return total + rotated(total, 64, 2)

    fsend[0] = end_face(v3, 7, 2).reshape(LAYER, 128)
    fsend[1] = end_face(v3, 4, 3).reshape(LAYER, 128)
    face_copies = [
        remote(fsend.at[0], frecv.at[0], f3send.at[0], f3recv.at[0], (grp, up)),
        remote(fsend.at[1], frecv.at[1], f3send.at[1], f3recv.at[1], (grp, down)),
    ]
    for copy in face_copies:
        copy.start()

    whole = remote(red.at[1:DOMS], red.at[1:DOMS], rsend, rrecv, (grp, up))
    whole.wait_send()
    whole.wait_recv()

    total = jnp.sum(red[...], axis=0)
    total = jnp.broadcast_to(jnp.sum(total, axis=1, keepdims=True), (8, 128))
    moments[...] = total

    def scalar(row):
        return jnp.broadcast_to(moments[row : row + 1, :], (8, 128))

    alpha = [scalar(row) for row in range(4)]
    beta = [scalar(4 + row) for row in range(4)]
    gamma = [(alpha[k] - THETA * beta[k]) * (1.0 / DELTA) for k in range(4)]
    mu = [beta[0], gamma[0]]
    ahead = gamma[0]
    for k in range(1, 4):
        ahead = 2.0 * gamma[k] - ahead
        mu.append(2.0 * beta[k] - mu[0])
        mu.append(2.0 * ahead - mu[1])

    def inner(i, j):
        return 0.5 * (mu[i + j] + mu[abs(i - j)])

    gram = [
        [
            DELTA * 0.5 * (inner(i, j + 1) + inner(i, abs(j - 1))) + THETA * inner(i, j)
            for j in range(4)
        ]
        for i in range(4)
    ]
    right = [mu[k] for k in range(4)]
    pivots = []
    for k in range(4):
        original = DELTA * 0.5 * (inner(k, k + 1) + inner(k, abs(k - 1))) + THETA * inner(k, k)
        pivot = gram[k][k]
        good = pivot > 1e-7 * original
        inverse = jnp.where(good, 1.0 / jnp.where(good, pivot, 1.0), 0.0)
        pivots.append(inverse)
        for i in range(k + 1, 4):
            factor = gram[i][k] * inverse
            for j in range(k + 1, 4):
                gram[i][j] = gram[i][j] - factor * gram[k][j]
            right[i] = right[i] - factor * right[k]
    coef = [None] * 4
    for k in (3, 2, 1, 0):
        value = right[k]
        for j in range(k + 1, 4):
            value = value - gram[k][j] * coef[j]
        coef[k] = value * pivots[k]
    wide = [value.reshape(1, 8, 128) for value in coef]

    for copy in face_copies:
        copy.wait()

    def combine(layer, tile, count):
        value = wide[0] * load(v0, layer, tile)
        for k in range(1, count):
            value = value + wide[k] * load(basis[k], layer, tile)
        return value

    def solve_layer(layer):
        for tile in every:
            value = combine(layer, tile, 4)
            store(xs, layer - 4, tile, value)
            store_lhs(xlhs, layer - 4, tile, value)

    over(4, 8, solve_layer)

    def neighbour_face(layer, row, extra):
        total = combine(layer, 0, 3) * table(row, 0)
        for tile in (1, 2, 3):
            total = total + combine(layer, tile, 3) * table(row, tile)
        total = total + rotated(total, 64, 2)
        return total + wide[3] * extra.reshape(8, 8, 128)

    fbuf[0] = neighbour_face(3, 2, frecv[0]).reshape(LAYER, 128)
    fbuf[1] = neighbour_face(8, 3, frecv[1]).reshape(LAYER, 128)

    def in_plane(tile, carry):
        start = pl.multiple_of(tile * 128, 128)
        left = jnp.concatenate(
            [xlhs[:, pl.ds(part * NODES + start, 128)] for part in range(3)], 1
        )
        both = jnp.dot(left, flat[...], preferred_element_type=F32)
        gx[:, pl.ds(start, 128)] = both[:, 0:128]
        gy[:, pl.ds(start, 128)] = both[:, 128:256]
        return carry

    lax.fori_loop(0, 4, in_plane, 0)
    multiply(xlhs, 0, 4, 1, gz, 0)

    def put_grad(layer, direction, tile, value):
        base = direction * NODES + tile * 128
        packed_in[rows_of(layer), base : base + 128] = (
            (value * 0.125).reshape(LAYER, 128).astype(BF16)
        )

    packed_in = lhs
    x_face = x_high | x_low
    y_row = lax.broadcasted_iota(jnp.int32, (8, 8, 128), 0)
    y_face = (y_high & (y_row < 7)) | (y_low & (y_row > 0))

    def grad_layer(layer, z_low, z_high):
        for tile in every:
            value = load(gx, layer, tile)
            value = jnp.where(x_face, 0.5, 1.0) * (value + x_neighbours(value))
            put_grad(layer, 0, tile, value)
            value = load(gy, layer, tile)
            value = jnp.where(y_face, 0.5, 1.0) * (value + y_neighbours(value))
            put_grad(layer, 1, tile, value)
            value = load(gz, layer, tile)
            if tile == 0:
                if z_low is None:
                    other, there = load(gz, layer - 1, 3), 1.0
                    other = rotated(other, 64, 2)
                else:
                    other, there = z_low
                mixed = value + (0.5 * there) * (other - value)
                value = jnp.where(half_low, mixed, value)
            if tile == 3:
                if z_high is None:
                    other, there = load(gz, layer + 1, 0), 1.0
                    other = rotated(other, 64, 2)
                else:
                    other, there = z_high
                mixed = value + (0.5 * there) * (other - value)
                value = jnp.where(half_low, value, mixed)
            put_grad(layer, 2, tile, value)

    grad_layer(0, (fbuf[0].reshape(8, 8, 128), has_down), None)
    over(1, 3, lambda layer: grad_layer(layer, None, None))
    grad_layer(3, None, (fbuf[1].reshape(8, 8, 128), has_up))

    def pack(part, carry):
        cols = pl.ds(pl.multiple_of(part * 256, 256), 256)
        packed[:, cols] = jnp.dot(
            gpack[...], packed_in[0:CELLS, cols], preferred_element_type=F32
        ).astype(BF16)
        return carry

    lax.fori_loop(0, 6, pack, 0)

    def to_group(target, slot):
        start = pl.multiple_of(target * LAYER, LAYER)
        return remote(
            packed.at[pl.ds(start, LAYER)], recv.at[comp],
            asend.at[slot], arecv.at[comp], (target, dom),
        )

    def each_send(action):
        @pl.when(grp < 2)
        def _():
            for step in range(1, 4):
                action(to_group(lax.rem(grp + step, 4), step - 1))

        @pl.when(grp >= 2)
        def _():
            action(to_group(3 - grp, 0))

    each_send(lambda copy: copy.start())
    recv[comp] = packed[pl.ds(pl.multiple_of(grp * LAYER, LAYER), LAYER), :]

    def velocity_out(tile, carry):
        cols = pl.ds(pl.multiple_of(tile * 128, 128), 128)
        total = jnp.zeros((CELLS, 128), F32)
        for part in split3(xs[:, cols]):
            total = total + jnp.dot(ptr[...], part, preferred_element_type=F32)
        out[:, cols] = total
        return carry

    @pl.when(grp < 3)
    def _():
        lax.fori_loop(0, 4, velocity_out, 0)

    each_send(lambda copy: copy.wait_send())
    for step in (1, 2):
        other = lax.rem(comp + step, 3)
        remote(recv.at[other], recv.at[other], asend.at[0], arecv.at[other], (grp, up)).wait_recv()

    def lambda_rows(block, carry):
        rows = pl.ds(pl.multiple_of(block * 16, 16), 16)
        for part in range(2):
            jac = [
                [
                    recv[c, rows, d * NODES + part * 256 : d * NODES + part * 256 + 256].astype(F32)
                    for d in range(3)
                ]
                for c in range(3)
            ]
            lam[rows, part * 256 : part * 256 + 256] = lambda_two(jac)
        return carry

    lax.fori_loop(0, 4, lambda_rows, 0)

    base = grp * 8
    here = pl.ds(pl.multiple_of(dom * 8, 8), 8)

    def to_owner(k):
        return remote(
            lam.at[8 * k : 8 * k + 8], lamrecv.at[here], osend.at[k], orecv, (3, base + k)
        )

    def each_owner(action):
        for k in range(8):
            own = (grp == 3) & (base + k == dom)

            @pl.when(jnp.logical_not(own))
            def _():
                action(to_owner(k))

    each_owner(lambda copy: copy.start())
    for k in range(8):

        @pl.when((grp == 3) & (base + k == dom))
        def _():
            lamrecv[here, :] = lam[8 * k : 8 * k + 8, :]

    each_owner(lambda copy: copy.wait_send())

    def wait_rows(count):
        piece = lamrecv.at[0 : 8 * count]
        remote(piece, piece, osend.at[0], orecv, (grp, up)).wait_recv()

    @pl.when((grp == 3) & (dom >= 24))
    def _():
        wait_rows(31)

    @pl.when((grp == 3) & (dom < 24))
    def _():
        wait_rows(32)

    @pl.when(grp == 3)
    def _():
        out[...] = lamrecv[...]


def lambda_two(jac):
    strain = [[0.5 * (jac[a][b] + jac[b][a]) for b in range(3)] for a in range(3)]
    spin = [[0.5 * (jac[a][b] - jac[b][a]) for b in range(3)] for a in range(3)]
    m = [[None] * 3 for _ in range(3)]
    for a in range(3):
        for b in range(a, 3):
            value = strain[a][0] * strain[0][b] + spin[a][0] * spin[0][b]
            for k in (1, 2):
                value = value + strain[a][k] * strain[k][b] + spin[a][k] * spin[k][b]
            m[a][b] = value
            m[b][a] = value
    for sweep in range(SWEEPS):
        for p, q, r in ((0, 1, 2), (0, 2, 1), (1, 2, 0)):
            last = sweep == SWEEPS - 1
            twice = 2.0 * m[p][q]
            gap = m[p][p] - m[q][q]
            square = twice * twice + gap * gap
            inverse = lax.rsqrt(jnp.maximum(square, 1e-36))
            length = square * inverse
            mean = 0.5 * (m[p][p] + m[q][q])
            m[p][p] = mean + 0.5 * length
            m[q][q] = mean - 0.5 * length
            if last and (p, q) == (1, 2):
                continue
            none = square < 1e-36
            cosine2 = jnp.where(none, 1.0, jnp.abs(gap) * inverse)
            sine2 = jnp.where(none, 0.0, twice * inverse)
            larger = 0.5 + 0.5 * cosine2
            root = lax.rsqrt(larger)
            big = larger * root
            small = 0.5 * sine2 * root
            flip = gap < 0.0
            sine_big = jnp.where(sine2 < 0.0, -big, big)
            cosine = jnp.where(flip, jnp.abs(small), big)
            sine = jnp.where(flip, sine_big, small)
            side_p = m[r][p]
            side_q = m[r][q]
            m[r][p] = m[p][r] = cosine * side_p + sine * side_q
            m[r][q] = m[q][r] = cosine * side_q - sine * side_p
            m[p][q] = m[q][p] = jnp.zeros_like(side_p)
    diagonal = [m[0][0], m[1][1], m[2][2]]
    largest = jnp.maximum(jnp.maximum(diagonal[0], diagonal[1]), diagonal[2])
    smallest = jnp.minimum(jnp.minimum(diagonal[0], diagonal[1]), diagonal[2])
    return diagonal[0] + diagonal[1] + diagonal[2] - largest - smallest


def per_device(forcing, viscosity, mass_coef, element_order, owner):
    mats, flat, lanes = tables()
    par_in = jnp.concatenate(
        [
            viscosity[None],
            mass_coef[None],
            element_order.astype(F32),
            jnp.zeros((5, CELLS), F32),
        ],
        0,
    )
    vmem = pl.BlockSpec(memory_space=pltpu.VMEM)
    anywhere = pl.BlockSpec(memory_space=pl.ANY)
    wide = (12 * LAYER, NODES)
    own = (CELLS, NODES)
    dma = pltpu.SemaphoreType.DMA
    result = pl.pallas_call(
        kernel,
        out_shape=jax.ShapeDtypeStruct(own, F32),
        in_specs=[anywhere, vmem, vmem, vmem, vmem, anywhere],
        out_specs=vmem,
        scratch_shapes=[
            pltpu.VMEM(own, F32),
            pltpu.VMEM((2, 3 * NODES, NODES), BF16),
            pltpu.VMEM((8, CELLS), F32),
            pltpu.VMEM((2, 8, CELLS), F32),
            pltpu.VMEM((CELLS, CELLS), BF16),
            pltpu.VMEM((CELLS, CELLS), BF16),
            pltpu.VMEM((12 * LAYER, 128), F32),
            pltpu.VMEM((12 * LAYER, 128), F32),
            pltpu.VMEM(wide, F32),
            pltpu.VMEM(wide, F32),
            pltpu.VMEM(wide, F32),
            pltpu.VMEM((12 * LAYER, 3 * NODES), BF16),
            pltpu.VMEM(wide, F32),
            pltpu.VMEM(wide, F32),
            pltpu.VMEM(wide, F32),
            pltpu.VMEM(wide, F32),
            pltpu.VMEM(own, F32),
            pltpu.VMEM((CELLS, 3 * NODES), BF16),
            pltpu.VMEM(own, F32),
            pltpu.VMEM(own, F32),
            pltpu.VMEM(own, F32),
            pltpu.VMEM((CELLS, CELLS), BF16),
            pltpu.VMEM((2, LAYER, 128), F32),
            pltpu.VMEM((2, LAYER, 128), F32),
            pltpu.VMEM((2, LAYER, 128), F32),
            pltpu.VMEM((8, 128), F32),
            pltpu.VMEM((DOMS, 8, 128), F32),
            pltpu.VMEM((CELLS, 3 * NODES), BF16),
            pltpu.VMEM((3, LAYER, 3 * NODES), BF16),
            pltpu.VMEM((LAYER, NODES), F32),
            pltpu.VMEM(own, F32),
            dma((6,)), dma, dma((2,)), dma((2,)), dma((4,)), dma((4,)), dma((2,)), dma((2,)),
            dma, dma, dma((3,)), dma((3,)), dma((8,)), dma,
        ],
        compiler_params=pltpu.CompilerParams(
            collective_id=0, has_side_effects=True, vmem_limit_bytes=48 * 1024 * 1024
        ),
        name="solve_and_analyse",
    )(forcing, par_in, owner, jnp.asarray(lanes), jnp.asarray(flat), jnp.asarray(mats))
    return result[None]


def solution(mesh):
    in_specs = (P(None, "dom", None), P("dom"), P("dom"), P("dom", None), P("dom", None))
    out_specs = P("grp", "dom", None)
    return jax.shard_map(
        per_device, mesh=mesh, in_specs=in_specs, out_specs=out_specs, check_vma=False
    )
```

profile of v0, /device:TPU:7, one launch (start us, length us, event | category | flops | bytes accessed | tf_op | source)
XLA Modules:
  0.0 71.7 jit_solution(2507714162943509692)
XLA Ops:
  0.0 0.1 pad.3.clone
  0.1 0.7 convert_element_type.3
  0.8 0.8 %maximum_maximum_fusion.par_in = f32[8,256]{1,0:T(8,128)S(1)} fusion(f32[1,256]{1,0:T(1,128)S(1)} %convert_element_type.3, f32[1,256]{1,0:T(1,128)} %bitcast.4, f32[1,256]{1,0:T(1,128)} %bitcast.5, f32[8]{0:T(128)S(1)} %pad.3.clone), kind=kLoop, calls=%fused_computation | loop fusion | flops 6144 | bytes 11296 | tf_op jit(solution)/shard_map/concatenate | solution.py:704
  1.5 0.0 copy-start
  1.5 1.6 %copy-done = bf16[2,2,512,512]{3,2,1,0:T(8,128)(2,1)S(1)} copy-done((bf16[2,2,512,512]{3,2,1,0:T(8,128)(2,1)S(1)}, bf16[2,2,512,512]{3,2,1,0:T(8,128)(2,1)}, u32[]{:S(2)}) %copy-start) | copy-done | bytes 2097176
  3.1 0.0 copy-start.1
  3.1 1.4 %copy-done.1 = f32[3,256,512]{2,1,0:T(8,128)S(1)} copy-done((f32[3,256,512]{2,1,0:T(8,128)S(1)}, f32[3,256,512]{2,1,0:T(8,128)}, u32[]{:S(2)}) %copy-start.1) | copy-done | bytes 1572888
  4.5 0.0 copy-start.2
  4.5 0.9 %copy-done.2 = bf16[384,256]{1,0:T(8,128)(2,1)S(1)} copy-done((bf16[384,256]{1,0:T(8,128)(2,1)S(1)}, bf16[384,256]{1,0:T(8,128)(2,1)}, u32[]{:S(2)}) %copy-start.2) | copy-done | bytes 196632
  5.5 0.0 copy-start.3
  5.5 0.7 copy-done.3
  6.2 0.0 copy-start.4
  6.2 0.7 copy-done.4
  6.9 64.1 %solve_and_analyse.1 = f32[256,512]{1,0:T(8,128)S(1)} custom-call(f32[3,256,512]{2,1,0:T(8,128)S(1)} %copy-done.1, f32[8,256]{1,0:T(8,128)S(1)} %maximum_maximum_fusion.par_in, s32[1,256]{1,0:T(1,128)S(1)} %copy-done.4, f32[8,512]{1,0:T(8,128)S(1)} %copy-done.3, bf16[384,256]{1,0:T(8,128)(2,1)S(1)} %copy-done.2, bf16[2,2,512,512]{3,2,1,0:T(8,128)(2,1)S(1)} %copy-done), custom_call_target="tpu_custom_call" | custom-call | tf_op jit(solution)/shard_map/solve_and_analyse/pallas_call | solution.py:718
  71.0 0.8 %copy.10 = f32[1,256,512]{2,1,0:T(8,128)} copy(f32[1,256,512]{2,1,0:T(8,128)S(1)} %bitcast.3) | data formatting | bytes 1048576
  (1 shorter events, 0.0 us)
Async XLA Ops:
  1.5 1.6 %copy-start = (bf16[2,2,512,512]{3,2,1,0:T(8,128)(2,1)S(1)}, bf16[2,2,512,512]{3,2,1,0:T(8,128)(2,1)}, u32[]{:S(2)}) copy-start(bf16[2,2,512,512]{3,2,1,0:T(8,128)(2,1)} %constant.10.clone.mats) | copy-start | bytes 6291460
  3.1 1.4 %copy-start.1 = (f32[3,256,512]{2,1,0:T(8,128)S(1)}, f32[3,256,512]{2,1,0:T(8,128)}, u32[]{:S(2)}) copy-start(f32[3,256,512]{2,1,0:T(8,128)} %forcing.1) | copy-start | bytes 4718596
  4.5 0.9 %copy-start.2 = (bf16[384,256]{1,0:T(8,128)(2,1)S(1)}, bf16[384,256]{1,0:T(8,128)(2,1)}, u32[]{:S(2)}) copy-start(bf16[384,256]{1,0:T(8,128)(2,1)} %constant.9.clone.flat) | copy-start | bytes 589828
  5.5 0.7 copy-start.3
  6.2 0.7 copy-start.4
where the time goes:
time: 72.7 us; the launch traced here: 71.7 us
  Pallas kernels  64.1 us (88%)
  local copies, waits for them, and re-layouts  6.19 us (9%)
  other arithmetic  1.45 us (2%)
    pallas_call x1, Pallas kernels, per_device(): pl.pallas_call(kernel, out_shape=jax.ShapeDtypeStruct(own, F32), in_specs...  64.1 us
    unnamed x11, local copies, waits for them, and re-layouts  6.12 us

commit v1 on v0

--- a/solution.py
+++ b/solution.py
@@ -93,11 +93,11 @@
 
 
 def kernel(
-    forcing, par_in, owner_in, lanes, flat, mats,
+    forcing, visc_in, mass_in, order_in, owner_in, lanes_in, flat_in, mats,
     out,
-    fsc, weights, par, parn, pone, ptr, visc, mass, raw, tmp, inv, lhs, v0, v1, v2, v3,
+    fsc, lanes, flat, order_sc, owner_sc, weights, par, parn, pone, ptr, visc, mass, raw, tmp, inv, lhs, v0, v1, v2, v3,
     xs, xlhs, gx, gy, gz, gpack, fbuf, fsend, frecv, moments, red, packed, recv, lam, lamrecv,
-    wsem, fsem, psend, precv, gsend, grecv, f3send, f3recv, rsend, rrecv, asend, arecv,
+    ssem, wsem, fsem, psend, precv, gsend, grecv, f3send, f3recv, rsend, rrecv, asend, arecv,
     osend, orecv,
 ):
     grp = lax.axis_index("grp")
@@ -116,9 +116,24 @@
             barrier, inc=1, device_id=(lax.rem(grp + step, 4), dom), device_id_type=MESH
         )
 
+    load_small = [
+        pltpu.make_async_copy(source, target, ssem.at[k])
+        for k, (source, target) in enumerate(
+            (
+                (visc_in, par.at[0:1]),
+                (mass_in, par.at[1:2]),
+                (order_in, order_sc),
+                (owner_in, owner_sc),
+                (lanes_in, lanes),
+            )
+        )
+    ]
+    for copy in load_small:
+        copy.start()
     load_force = pltpu.make_async_copy(forcing.at[comp], fsc, fsem)
     load_force.start()
-    load_mats = []
+    load_mats = [pltpu.make_async_copy(flat_in, flat, wsem.at[6])]
+    load_mats[0].start()
     for which in range(2):
         for part, source in enumerate((0, 0, 1)):
             copy = pltpu.make_async_copy(
@@ -188,7 +203,10 @@
 
     cell_sub = lax.broadcasted_iota(jnp.int32, (CELLS, CELLS), 0).astype(F32)
     cell_lane = lax.broadcasted_iota(jnp.int32, (CELLS, CELLS), 1).astype(F32)
-    par[...] = par_in[...]
+    for copy in load_small:
+        copy.wait()
+    par[2:3, :] = order_sc[...].astype(F32)
+    par[3:8, :] = jnp.zeros((5, CELLS), F32)
 
     def coefficients(ref, base, scale):
         hit = ref[2:3, :] == cell_sub
@@ -267,7 +285,7 @@
     every = (0, 1, 2, 3)
     over(4, 8, lambda layer: assemble_xy(layer, every, None))
 
-    owner_row = owner_in[...].astype(F32)
+    owner_row = owner_sc[...].astype(F32)
     owner_col = jnp.sum(
         jnp.where(cell_sub == cell_lane, owner_row, 0.0), axis=1, keepdims=True
     )
@@ -701,27 +719,22 @@
 
 def per_device(forcing, viscosity, mass_coef, element_order, owner):
     mats, flat, lanes = tables()
-    par_in = jnp.concatenate(
-        [
-            viscosity[None],
-            mass_coef[None],
-            element_order.astype(F32),
-            jnp.zeros((5, CELLS), F32),
-        ],
-        0,
-    )
     vmem = pl.BlockSpec(memory_space=pltpu.VMEM)
-    anywhere = pl.BlockSpec(memory_space=pl.ANY)
+    hbm = pl.BlockSpec(memory_space=pltpu.HBM)
     wide = (12 * LAYER, NODES)
     own = (CELLS, NODES)
     dma = pltpu.SemaphoreType.DMA
     result = pl.pallas_call(
         kernel,
         out_shape=jax.ShapeDtypeStruct(own, F32),
-        in_specs=[anywhere, vmem, vmem, vmem, vmem, anywhere],
+        in_specs=[hbm] * 8,
         out_specs=vmem,
         scratch_shapes=[
             pltpu.VMEM(own, F32),
+            pltpu.VMEM((8, NODES), F32),
+            pltpu.VMEM((384, 256), BF16),
+            pltpu.VMEM((1, CELLS), jnp.int32),
+            pltpu.VMEM((1, CELLS), jnp.int32),
             pltpu.VMEM((2, 3 * NODES, NODES), BF16),
             pltpu.VMEM((8, CELLS), F32),
             pltpu.VMEM((2, 8, CELLS), F32),
@@ -752,14 +765,17 @@
             pltpu.VMEM((3, LAYER, 3 * NODES), BF16),
             pltpu.VMEM((LAYER, NODES), F32),
             pltpu.VMEM(own, F32),
-            dma((6,)), dma, dma((2,)), dma((2,)), dma((4,)), dma((4,)), dma((2,)), dma((2,)),
+            dma((5,)), dma((7,)), dma, dma((2,)), dma((2,)), dma((4,)), dma((4,)), dma((2,)), dma((2,)),
             dma, dma, dma((3,)), dma((3,)), dma((8,)), dma,
         ],
         compiler_params=pltpu.CompilerParams(
-            collective_id=0, has_side_effects=True, vmem_limit_bytes=48 * 1024 * 1024
+            collective_id=0, has_side_effects=True, vmem_limit_bytes=60 * 1024 * 1024
         ),
         name="solve_and_analyse",
-    )(forcing, par_in, owner, jnp.asarray(lanes), jnp.asarray(flat), jnp.asarray(mats))
+    )(
+        forcing, viscosity[None], mass_coef[None], element_order, owner,
+        jnp.asarray(lanes), jnp.asarray(flat), jnp.asarray(mats),
+    )
     return result[None]
 
 

time: 72.7 us -> 67.6 us (0.930); the launches traced: 71.7 us -> 67.5 us
  local copies, waits for them, and re-layouts: 6.19 us -> 1.87 us
  Pallas kernels: 64.1 us -> 65.6 us
  other arithmetic: 1.45 us -> 0 us
    unnamed x11 -> x1, local copies, waits for them, and re-layouts: 6.12 us -> 1.87 us
    pallas_call x1, Pallas kernels: 64.1 us -> 65.6 us  [per_device(): pl.pallas_call(kernel, out_shape=jax.ShapeDtypeStruct(own, F32), in_specs...]
    concatenate x1 -> x0, other arithmetic: 0.76 us -> none  [per_device(): jnp.concatenate([viscosity[None], mass_coef[None], element_order.astype(F...]
where the time goes in v1:
time: 67.6 us; the launch traced here: 67.5 us
  Pallas kernels  65.6 us (97%)
  local copies, waits for them, and re-layouts  1.87 us (3%)
    pallas_call x1, Pallas kernels, per_device(): pl.pallas_call(kernel, out_shape=jax.ShapeDtypeStruct(own, F32), in_specs...  65.6 us
    unnamed x1, local copies, waits for them, and re-layouts  1.87 us

profile of v1, /device:TPU:7, one launch (start us, length us, event | category | flops | bytes accessed | tf_op | source)
XLA Modules:
  0.0 67.5 jit_solution(3475356705196866220)
XLA Ops:
  0.0 65.6 %solve_and_analyse.1 = f32[256,512]{1,0:T(8,128)} custom-call(f32[3,256,512]{2,1,0:T(8,128)} %forcing.1, f32[1,256]{1,0:T(1,128)} %bitcast.4, f32[1,256]{1,0:T(1,128)} %bitcast.5, s32[1,256]{1,0:T(1,128)} %order_in.1, s32[1,256]{1,0:T(1,128)} %owner_in.1, f32[8,512]{1,0:T(8,128)} %constant.6.clone.lanes_in, bf16[384,256]{1,0:T(8,128)(2,1)} %constant.7.clone.flat_in, ...), custom_call_target="tpu_custom_call" | custom-call | tf_op jit(solution)/shard_map/solve_and_analyse/pallas_call | solution.py:727
  65.6 1.9 %copy.10 = f32[1,256,512]{2,1,0:T(8,128)} copy(f32[1,256,512]{2,1,0:T(8,128)} %bitcast.3) | data formatting | bytes 1048576

commit v2 on v1

--- a/solution.py
+++ b/solution.py
@@ -83,9 +83,18 @@
     lanes = np.zeros((8, NODES), np.float32)
     lanes[0] = cube
     lanes[1] = np.diag(stiff)
-    lanes[2] = np.repeat(diff[NP - 1], LAYER)
-    lanes[3] = np.repeat(diff[0], LAYER)
-    return mats, flat, lanes
+    lanes[2] = np.repeat(diff[0], LAYER)
+    back = eye[::-1]
+    half = np.eye(2)
+    mirror = np.concatenate(
+        [
+            np.kron(half, np.kron(eye, back)),
+            np.kron(half, np.kron(back, eye)),
+            np.kron(half, np.kron(back, back)),
+        ],
+        1,
+    ).astype(ml_dtypes.bfloat16)
+    return mats, np.concatenate([np.concatenate([flat, np.zeros((384, 128), flat.dtype)], 1), mirror], 0), lanes
 
 
 def rotated(value, shift, axis):
@@ -95,8 +104,9 @@
 def kernel(
     forcing, visc_in, mass_in, order_in, owner_in, lanes_in, flat_in, mats,
     out,
-    fsc, lanes, flat, order_sc, owner_sc, weights, par, parn, pone, ptr, visc, mass, raw, tmp, inv, lhs, v0, v1, v2, v3,
-    xs, xlhs, gx, gy, gz, gpack, fbuf, fsend, frecv, moments, red, packed, recv, lam, lamrecv,
+    fsc, lanes, flat, order_sc, owner_sc, weights, par, parn, pone, ptr, visc, mass, raw, tmp,
+    inv, lhs, v0, v1, v2, v3, xs, xstd, grads, gz, gpack, classes, gcells, fsend, frecv, moments,
+    red, packed, recv, lam, lamrecv,
     ssem, wsem, fsem, psend, precv, gsend, grecv, f3send, f3recv, rsend, rrecv, asend, arecv,
     osend, orecv,
 ):
@@ -106,6 +116,8 @@
     up = lax.rem(dom + 1, DOMS)
     down = lax.rem(dom + DOMS - 1, DOMS)
     barrier = pltpu.get_barrier_semaphore()
+    basis = (v0, v1, v2, v3)
+    every = (0, 1, 2, 3)
 
     for step in range(1, DOMS):
         pl.semaphore_signal(
@@ -125,6 +137,7 @@
                 (order_in, order_sc),
                 (owner_in, owner_sc),
                 (lanes_in, lanes),
+                (flat_in, flat),
             )
         )
     ]
@@ -132,8 +145,7 @@
         copy.start()
     load_force = pltpu.make_async_copy(forcing.at[comp], fsc, fsem)
     load_force.start()
-    load_mats = [pltpu.make_async_copy(flat_in, flat, wsem.at[6])]
-    load_mats[0].start()
+    load_mats = []
     for which in range(2):
         for part, source in enumerate((0, 0, 1)):
             copy = pltpu.make_async_copy(
@@ -144,34 +156,48 @@
             copy.start()
             load_mats.append(copy)
 
-    lane = lax.broadcasted_iota(jnp.int32, (8, 8, 128), 2)
-    sub = lax.broadcasted_iota(jnp.int32, (8, 8, 128), 1)
+    lane = lax.broadcasted_iota(jnp.int32, (8, 128), 1)
+    sub = lax.broadcasted_iota(jnp.int32, (8, 128), 0)
     node_i = lax.rem(lane, 8)
     node_j = lax.rem(lane // 8, 8)
-    x_high = (node_i == 7) & (sub < 7)
-    x_low = (node_i == 0) & (sub > 0)
-    y_high = node_j == 7
-    y_low = node_j == 0
-    half_low = lane < LAYER
+    odd = lax.rem(sub, 2) == 1
+    first_i = node_i == 0
+    last_i = node_i == 7
+    take_up = ((last_i & jnp.logical_not(odd)) | (first_i & odd & (sub < 7)))
+    take_down = ((last_i & odd) | (first_i & jnp.logical_not(odd) & (sub > 0)))
     has_up = jnp.where(dom < DOMS - 1, 1.0, 0.0).astype(F32)
     has_down = jnp.where(dom > 0, 1.0, 0.0).astype(F32)
 
-    def x_neighbours(a):
-        above = rotated(rotated(a, 7, 2), -1, 1)
-        below = rotated(rotated(a, -7, 2), 1, 1)
-        return jnp.where(x_high, above, jnp.where(x_low, below, 0.0))
-
-    def y_neighbours(a):
+    def wide(mask):
+        return jnp.broadcast_to(mask[None], (8, 8, 128))
+
+    x_up = wide(take_up)
+    x_down = wide(take_down)
+    x_odd = wide(odd)
+    y_last = wide(node_j == 7)
+    y_first = wide(node_j == 0)
+    low_half = wide(lane < LAYER)
+
+    def x_others(a):
+        above = rotated(a, -1, 1)
+        below = rotated(a, 1, 1)
+        return jnp.where(x_up, above, jnp.where(x_down, below, 0.0))
+
+    def y_others(a):
         blank = jnp.zeros((1, 8, 128), F32)
-        above = jnp.concatenate([rotated(a, 56, 2)[1:], blank], 0)
-        below = jnp.concatenate([blank, rotated(a, -56, 2)[:-1]], 0)
-        return jnp.where(y_high, above, jnp.where(y_low, below, 0.0))
+        last = jnp.concatenate([a[k ^ 1 : (k ^ 1) + 1] for k in range(8)], 0)
+        first = jnp.concatenate(
+            [blank] + [a[k : k + 1] for k in (2, 1, 4, 3, 6, 5)] + [blank], 0
+        )
+        return jnp.where(y_last, last, jnp.where(y_first, first, 0.0))
 
     def xy_sum(a):
-        a = a + x_neighbours(a)
-        return a + y_neighbours(a)
+        a = a + x_others(a)
+        return a + y_others(a)
 
     def rows_of(layer):
+        if isinstance(layer, int):
+            return slice(layer * LAYER, layer * LAYER + LAYER)
         return pl.ds(pl.multiple_of(layer * LAYER, LAYER), LAYER)
 
     def load(ref, layer, tile):
@@ -193,13 +219,40 @@
         low = (rest - middle.astype(F32)).astype(BF16)
         return high, middle, low
 
-    def store_lhs(ref, layer, tile, value):
+    def store_lhs(layer, tile, value):
         value = value.reshape(LAYER, 128)
         high = value.astype(BF16)
         low = (value - high.astype(F32)).astype(BF16)
-        ref[rows_of(layer), tile * 128 : tile * 128 + 128] = high
-        ref[rows_of(layer), NODES + tile * 128 : NODES + tile * 128 + 128] = low
-        ref[rows_of(layer), 2 * NODES + tile * 128 : 2 * NODES + tile * 128 + 128] = high
+        lhs[rows_of(layer), tile * 128 : tile * 128 + 128] = high
+        lhs[rows_of(layer), NODES + tile * 128 : NODES + tile * 128 + 128] = low
+        lhs[rows_of(layer), 2 * NODES + tile * 128 : 2 * NODES + tile * 128 + 128] = high
+
+    def reversals(value):
+        total = None
+        for part in split3(value):
+            term = jnp.dot(part, flat[384:512, :], preferred_element_type=F32)
+            total = term if total is None else total + term
+        return total[:, 0:128], total[:, 128:256], total[:, 256:384]
+
+    def mirror_layers(value, tile, target, base):
+        flipped = reversals(value)
+        for layer in range(4):
+            rows = slice(layer * LAYER, layer * LAYER + LAYER)
+            plain, rev_x, rev_y, rev_xy = [
+                part[rows].reshape(8, 8, 128) for part in (value,) + flipped
+            ]
+            even_y = jnp.where(x_odd, rev_x, plain)
+            odd_y = jnp.where(x_odd, rev_xy, rev_y)
+            mixed = jnp.concatenate(
+                [(odd_y if k % 2 else even_y)[k : k + 1] for k in range(8)], 0
+            )
+            if layer % 2:
+                store(target, base + layer, 3 - tile, rotated(mixed, 64, 2))
+            else:
+                store(target, base + layer, tile, mixed)
+
+    def over(low, high, body):
+        lax.fori_loop(low, high, lambda layer, carry: (body(layer), carry)[1], 0)
 
     cell_sub = lax.broadcasted_iota(jnp.int32, (CELLS, CELLS), 0).astype(F32)
     cell_lane = lax.broadcasted_iota(jnp.int32, (CELLS, CELLS), 1).astype(F32)
@@ -215,25 +268,15 @@
             target[base : base + CELLS, :] = jnp.broadcast_to(col * scale, (CELLS, 128))
         return hit
 
-    hit = coefficients(par, CELLS, 1.0)
-    pone[...] = jnp.where(hit, 1.0, 0.0).astype(BF16)
-    order_col = jnp.sum(
-        jnp.where(cell_sub == cell_lane, par[2:3, :], 0.0), axis=1, keepdims=True
-    )
-    ptr[...] = jnp.where(order_col == cell_lane, 1.0, 0.0).astype(BF16)
-
+    pone[...] = jnp.where(par[2:3, :] == cell_sub, 1.0, 0.0).astype(BF16)
     load_force.wait()
-
-    def gather_own(tile, carry):
-        cols = pl.ds(pl.multiple_of(tile * 128, 128), 128)
-        parts = split3(fsc[:, cols])
-        total = jnp.zeros((CELLS, 128), F32)
-        for part in parts:
-            total = total + jnp.dot(pone[...], part, preferred_element_type=F32)
-        raw[CELLS : 2 * CELLS, cols] = total * lanes[0:1, cols]
-        return carry
-
-    lax.fori_loop(0, 4, gather_own, 0)
+    for tile in every:
+        cols = slice(tile * 128, tile * 128 + 128)
+        total = None
+        for part in split3(fsc[:, cols]):
+            term = jnp.dot(pone[...], part, preferred_element_type=F32)
+            total = term if total is None else total + term
+        mirror_layers(total * lanes[0:1, cols], tile, raw, 4)
 
     pl.semaphore_wait(barrier, DOMS - 1 + 3)
 
@@ -261,30 +304,18 @@
             gsend.at[2], grecv.at[2], (grp, up),
         ),
         remote(
-            raw.at[7 * LAYER : 8 * LAYER, 0:128], raw.at[11 * LAYER : 12 * LAYER, 0:128],
+            raw.at[7 * LAYER : 8 * LAYER, 384:512], raw.at[11 * LAYER : 12 * LAYER, 384:512],
             gsend.at[3], grecv.at[3], (grp, down),
         ),
     ]
     for copy in par_copies + ghost_copies:
         copy.start()
 
-    def assemble_xy(layer, tiles, scale):
-        coef_v = column(visc, layer)
-        coef_m = column(mass, layer)
-        for tile in tiles:
-            force = load(raw, layer, tile)
-            if scale is not None:
-                force = force * scale
-            store(tmp, layer, tile, xy_sum(force))
-            diag = coef_v * table(1, tile) + coef_m * table(0, tile)
-            store(inv, layer, tile, xy_sum(diag))
-
-    def over(low, high, body):
-        lax.fori_loop(low, high, lambda layer, carry: (body(layer), carry)[1], 0)
-
-    every = (0, 1, 2, 3)
-    over(4, 8, lambda layer: assemble_xy(layer, every, None))
-
+    coefficients(par, CELLS, 1.0)
+    order_col = jnp.sum(
+        jnp.where(cell_sub == cell_lane, par[2:3, :], 0.0), axis=1, keepdims=True
+    )
+    ptr[...] = jnp.where(order_col == cell_lane, 1.0, 0.0).astype(BF16)
     owner_row = owner_sc[...].astype(F32)
     owner_col = jnp.sum(
         jnp.where(cell_sub == cell_lane, owner_row, 0.0), axis=1, keepdims=True
@@ -294,53 +325,89 @@
     dest_row = jnp.where(owner_row >= 0.0, owner_row * 8.0 + rank_row, -1.0)
     slot_of = jnp.where(dest_row == cell_sub, 1.0, 0.0).astype(BF16)
     gpack[...] = jnp.dot(slot_of, ptr[...], preferred_element_type=F32).astype(BF16)
+    cell_id = lax.broadcasted_iota(jnp.int32, (CELLS, 128), 0)
+    for k, width in enumerate((1, 8, 64)):
+        parity = lax.rem(cell_id // width, 2).astype(F32).astype(BF16)
+        classes[:, k * 128 : k * 128 + 128] = jnp.dot(
+            gpack[...], parity, preferred_element_type=F32
+        )
 
     for copy in par_copies:
         copy.wait()
     coefficients(parn.at[0], 0, has_down)
     coefficients(parn.at[1], 2 * CELLS, has_up)
+
+    def partners(layer):
+        parity = layer % 2 if isinstance(layer, int) else lax.rem(layer, 2)
+        return {0: layer - 1 + 2 * parity, 3: layer + 1 - 2 * parity}
+
+    def face_sum(ref, layer, tile):
+        value = load(ref, layer, tile)
+        other = load(ref, partners(layer)[tile], tile)
+        if tile == 0:
+            return value + jnp.where(low_half, other, 0.0)
+        return value + jnp.where(low_half, 0.0, other)
+
+    def put_inverse(layer, tile, diag):
+        store(inv, layer, tile, jnp.where(diag > 0.0, (2.0 / DELTA) / diag, 0.0))
+
+    def diagonal(layer, tiles):
+        coef_v = column(visc, layer)
+        coef_m = column(mass, layer)
+        for tile in tiles:
+            diag = xy_sum(coef_v * table(1, tile) + coef_m * table(0, tile))
+            if tile in (0, 3):
+                store(tmp, layer, tile, diag)
+            else:
+                put_inverse(layer, tile, diag)
+
+    diagonal(0, (3,))
+    over(1, 11, lambda layer: diagonal(layer, every))
+    diagonal(11, (3,))
+
+    def diagonal_faces(layer):
+        for tile in (0, 3):
+            put_inverse(layer, tile, face_sum(tmp, layer, tile))
+
+    over(1, 11, diagonal_faces)
+
+    def put_first(layer, tile, force):
+        value = force * load(inv, layer, tile) * (0.5 * DELTA)
+        store(v0, layer, tile, value)
+        store_lhs(layer, tile, value)
+
+    def assemble(layer, tiles, scale):
+        for tile in tiles:
+            force = load(raw, layer, tile)
+            if scale is not None:
+                force = force * scale
+            force = xy_sum(force)
+            if tile in (0, 3):
+                store(tmp, layer, tile, force)
+            else:
+                put_first(layer, tile, force)
+
+    over(4, 8, lambda layer: assemble(layer, every, None))
+    for copy in load_mats:
+        copy.wait()
     for copy in ghost_copies:
         copy.wait()
-
-    assemble_xy(0, (3,), has_down)
-    over(1, 4, lambda layer: assemble_xy(layer, every, has_down))
-    over(8, 11, lambda layer: assemble_xy(layer, every, has_up))
-    assemble_xy(11, (0,), has_up)
-
-    def z_sum(ref, layer, tile):
-        value = load(ref, layer, tile)
-        if tile == 0:
-            value = value + jnp.where(half_low, rotated(load(ref, layer - 1, 3), 64, 2), 0.0)
-        if tile == 3:
-            value = value + jnp.where(half_low, 0.0, rotated(load(ref, layer + 1, 0), 64, 2))
-        return value
-
-    def assemble_z(layer):
-        for tile in every:
-            diag = z_sum(inv, layer, tile)
-            force = z_sum(tmp, layer, tile)
-            inverse = jnp.where(diag > 0.0, 1.0 / jnp.where(diag > 0.0, diag, 1.0), 0.0)
-            store(v1, layer, tile, inverse)
-            value = force * inverse
-            store(v0, layer, tile, value)
-            store_lhs(lhs, layer, tile, value)
-
-    over(1, 11, assemble_z)
-
-    def copy_inverse(layer):
-        for tile in every:
-            store(inv, layer, tile, load(v1, layer, tile) * (1.0 / DELTA))
-
-    over(2, 10, copy_inverse)
-
-    for copy in load_mats:
-        copy.wait()
-
-    def multiply(left, low, high, which, target, target_low):
+    assemble(0, (3,), has_down)
+    over(1, 4, lambda layer: assemble(layer, every, has_down))
+    over(8, 11, lambda layer: assemble(layer, every, has_up))
+    assemble(11, (3,), has_up)
+
+    def first_faces(layer):
+        for tile in (0, 3):
+            put_first(layer, tile, face_sum(tmp, layer, tile))
+
+    over(1, 11, first_faces)
+
+    def multiply(low, high, which, target, target_low):
         def body(half, carry):
             cols = pl.ds(pl.multiple_of(half * 256, 256), 256)
             target[target_low * LAYER : (target_low + high - low) * LAYER, cols] = jnp.dot(
-                left[low * LAYER : high * LAYER, :],
+                lhs[low * LAYER : high * LAYER, :],
                 weights[which, :, cols],
                 preferred_element_type=F32,
             )
@@ -348,91 +415,152 @@
 
         lax.fori_loop(0, 2, body, 0)
 
-    def apply_xy(vec, layer, sums):
+    def advance(step, layer, tile, total):
+        value = total * load(inv, layer, tile)
+        current = load(basis[step], layer, tile)
+        if step == 0:
+            value = 0.5 * value - (THETA / DELTA) * current
+        else:
+            value = value - (2.0 * THETA / DELTA) * current - load(basis[step - 1], layer, tile)
+        store(basis[step + 1], layer, tile, value)
+        store_lhs(layer, tile, value)
+
+    def apply(step, layer, tiles, sums, going):
         coef_v = column(visc, layer)
         coef_m = column(mass, layer)
-        for tile in every:
-            value = load(vec, layer, tile)
-            image = coef_v * load(tmp, layer, tile) + coef_m * (table(0, tile) * value)
+        for tile in tiles:
+            value = load(basis[step], layer, tile)
+            weighted = coef_m * table(0, tile)
+            image = coef_v * load(tmp, layer, tile) + weighted * value
             if sums is not None:
-                diag = coef_v * table(1, tile) + coef_m * table(0, tile)
+                diag = coef_v * table(1, tile) + weighted
                 sums = (
                     sums[0] + jnp.sum(value * image, axis=0),
                     sums[1] + jnp.sum(value * value * diag, axis=0),
                 )
-            store(tmp, layer, tile, xy_sum(image))
+            if going:
+                image = xy_sum(image)
+                if tile in (0, 3):
+                    store(tmp, layer, tile, image)
+                else:
+                    advance(step, layer, tile, image)
         return sums
 
-    def last_sums(vec, layer, sums):
-        coef_v = column(visc, layer)
-        coef_m = column(mass, layer)
-        for tile in every:
-            value = load(vec, layer, tile)
-            image = coef_v * load(tmp, layer, tile) + coef_m * (table(0, tile) * value)
-            diag = coef_v * table(1, tile) + coef_m * table(0, tile)
-            sums = (
-                sums[0] + jnp.sum(value * image, axis=0),
-                sums[1] + jnp.sum(value * value * diag, axis=0),
-            )
-        return sums
-
-    def advance(layer, current, previous, following):
-        for tile in every:
-            value = z_sum(tmp, layer, tile) * load(inv, layer, tile)
-            value = value - (THETA / DELTA) * load(current, layer, tile)
-            if previous is not None:
-                value = 2.0 * value - load(previous, layer, tile)
-            store(following, layer, tile, value)
-            store_lhs(lhs, layer, tile, value)
-
-    blank = (jnp.zeros((8, 128), F32), jnp.zeros((8, 128), F32))
-    basis = (v0, v1, v2, v3)
+    def faces(step, layer):
+        for tile in (0, 3):
+            advance(step, layer, tile, face_sum(tmp, layer, tile))
+
+    blank_sums = (jnp.zeros((8, 128), F32), jnp.zeros((8, 128), F32))
     for step in range(ITERS):
         low, high = 1 + step, 11 - step
-        multiply(lhs, low, high, 0, tmp, low)
-        if step + 1 < ITERS:
-            over(low, 4, lambda layer: apply_xy(basis[step], layer, None))
-            sums = lax.fori_loop(
-                4, 8, lambda layer, carry: apply_xy(basis[step], layer, carry), blank
-            )
-            over(8, high, lambda layer: apply_xy(basis[step], layer, None))
-        else:
-            sums = lax.fori_loop(
-                4, 8, lambda layer, carry: last_sums(basis[step], layer, carry), blank
-            )
+        going = step + 1 < ITERS
+        multiply(low, high, 0, tmp, low)
+        if going:
+            inward = 0 if low % 2 else 3
+            apply(step, low, (inward,), None, True)
+            over(low + 1, 4, lambda layer: apply(step, layer, every, None, True))
+        sums = lax.fori_loop(
+            4, 8, lambda layer, carry: apply(step, layer, every, carry, going), blank_sums
+        )
+        if going:
+            over(8, high - 1, lambda layer: apply(step, layer, every, None, True))
+            apply(step, high - 1, (inward,), None, True)
         moments[step : step + 1, :] = jnp.sum(sums[0], axis=0, keepdims=True)
         moments[4 + step : 5 + step, :] = jnp.sum(sums[1], axis=0, keepdims=True)
-        if step + 1 < ITERS:
-            over(
-                low + 1,
-                high - 1,
-                lambda layer: advance(
-                    layer, basis[step], basis[step - 1] if step else None, basis[step + 1]
-                ),
-            )
+        if going:
+            over(low + 1, high - 1, lambda layer: faces(step, layer))
 
     red[0] = moments[...]
-    sum_copies = []
     for step in range(1, DOMS):
-        copy = remote(
+        remote(
             moments, red.at[step], rsend, rrecv, (grp, lax.rem(dom + step, DOMS))
-        )
-        copy.start()
-
-    def end_face(ref, layer, row):
-        total = load(ref, layer, 0) * table(row, 0)
+        ).start()
+
+    def end_face(ref, layer):
+        total = load(ref, layer, 0) * table(2, 0)
         for tile in (1, 2, 3):
-            total = total + load(ref, layer, tile) * table(row, tile)
-        return total + rotated(total, 64, 2)
-
-    fsend[0] = end_face(v3, 7, 2).reshape(LAYER, 128)
-    fsend[1] = end_face(v3, 4, 3).reshape(LAYER, 128)
+            total = total + load(ref, layer, tile) * table(2, tile)
+        total = total + rotated(total, 64, 2)
+        return -total if layer % 2 else total
+
+    fsend[0] = end_face(v3, 7).reshape(LAYER, 128)
+    fsend[1] = end_face(v3, 4).reshape(LAYER, 128)
     face_copies = [
         remote(fsend.at[0], frecv.at[0], f3send.at[0], f3recv.at[0], (grp, up)),
         remote(fsend.at[1], frecv.at[1], f3send.at[1], f3recv.at[1], (grp, down)),
     ]
     for copy in face_copies:
         copy.start()
+
+    x_sign = jnp.where(odd, -1.0, 1.0).reshape(1, 8, 128)
+    x_scale = jnp.where(take_up | take_down, 0.5, 1.0).reshape(1, 8, 128) * x_sign
+    y_half = jnp.where((node_j == 7) | (node_j == 0), 0.5, 1.0).reshape(1, 8, 128)
+    y_end = jnp.where(node_j == 7, 0.5, 1.0).reshape(1, 8, 128)
+    y_scale = jnp.concatenate(
+        [y_end, -y_half, y_half, -y_half, y_half, -y_half, y_half, -y_end], 0
+    )
+
+    def refill(ref):
+        def body(layer):
+            for tile in every:
+                store_lhs(layer, tile, load(ref, layer, tile))
+
+        over(4, 8, body)
+
+    for index in range(ITERS):
+        vec = basis[index]
+        if index < ITERS - 1:
+            refill_needed = True
+        else:
+            refill_needed = True
+        if refill_needed:
+            refill(vec)
+        own_rows = slice(4 * LAYER, 8 * LAYER)
+
+        def in_plane(tile, carry, index=index):
+            start = pl.multiple_of(tile * 128, 128)
+            left = jnp.concatenate(
+                [lhs[own_rows, pl.ds(part * NODES + start, 128)] for part in range(3)], 1
+            )
+            both = jnp.dot(left, flat[0:384, 0:256], preferred_element_type=F32)
+            for layer in range(4):
+                rows = slice(layer * LAYER, layer * LAYER + LAYER)
+                value = both[rows, 0:128].reshape(8, 8, 128)
+                value = x_scale * (value - x_others(value))
+                grads[index, rows, pl.ds(start, 128)] = value.reshape(LAYER, 128)
+                value = both[rows, 128:256].reshape(8, 8, 128)
+                value = y_scale * (value - y_others(value))
+                grads[index, rows, pl.ds(NODES + start, 128)] = value.reshape(LAYER, 128)
+            return carry
+
+        lax.fori_loop(0, 4, in_plane, 0)
+        multiply(4, 8, 1, gz, 0)
+        if index == ITERS - 1:
+            for copy in face_copies:
+                copy.wait()
+        for layer in range(4):
+            sign = -1.0 if layer % 2 else 1.0
+            for tile in every:
+                value = load(gz, layer, tile) * sign
+                if tile == 0:
+                    if layer in (0, 3):
+                        side = 0 if layer == 0 else 1
+                        if index == ITERS - 1:
+                            other = frecv[side].reshape(8, 8, 128)
+                        else:
+                            other = end_face(vec, 3 if side == 0 else 8)
+                        there = 0.5 * (has_down if side == 0 else has_up)
+                    else:
+                        other = load(gz, 3 - layer, 0) * -sign
+                        there = 0.5
+                    value = value + jnp.where(low_half, there * (other - value), 0.0)
+                if tile == 3:
+                    other = load(gz, layer ^ 1, 3) * -sign
+                    value = value + jnp.where(low_half, 0.0, 0.5 * (other - value))
+                base = 2 * NODES + tile * 128
+                grads[index, layer * LAYER : layer * LAYER + LAYER, base : base + 128] = (
+                    value.reshape(LAYER, 128)
+                )
 
     whole = remote(red.at[1:DOMS], red.at[1:DOMS], rsend, rrecv, (grp, up))
     whole.wait_send()
@@ -484,94 +612,27 @@
         for j in range(k + 1, 4):
             value = value - gram[k][j] * coef[j]
         coef[k] = value * pivots[k]
-    wide = [value.reshape(1, 8, 128) for value in coef]
-
-    for copy in face_copies:
-        copy.wait()
-
-    def combine(layer, tile, count):
-        value = wide[0] * load(v0, layer, tile)
-        for k in range(1, count):
-            value = value + wide[k] * load(basis[k], layer, tile)
-        return value
-
-    def solve_layer(layer):
-        for tile in every:
-            value = combine(layer, tile, 4)
-            store(xs, layer - 4, tile, value)
-            store_lhs(xlhs, layer - 4, tile, value)
-
-    over(4, 8, solve_layer)
-
-    def neighbour_face(layer, row, extra):
-        total = combine(layer, 0, 3) * table(row, 0)
-        for tile in (1, 2, 3):
-            total = total + combine(layer, tile, 3) * table(row, tile)
-        total = total + rotated(total, 64, 2)
-        return total + wide[3] * extra.reshape(8, 8, 128)
-
-    fbuf[0] = neighbour_face(3, 2, frecv[0]).reshape(LAYER, 128)
-    fbuf[1] = neighbour_face(8, 3, frecv[1]).reshape(LAYER, 128)
-
-    def in_plane(tile, carry):
-        start = pl.multiple_of(tile * 128, 128)
-        left = jnp.concatenate(
-            [xlhs[:, pl.ds(part * NODES + start, 128)] for part in range(3)], 1
-        )
-        both = jnp.dot(left, flat[...], preferred_element_type=F32)
-        gx[:, pl.ds(start, 128)] = both[:, 0:128]
-        gy[:, pl.ds(start, 128)] = both[:, 128:256]
+
+    wide16 = [
+        jnp.concatenate([value * (1.0 / NP)] * 2, 0).reshape(1, 16, 128) for value in coef
+    ]
+
+    def combine_grads(block, carry):
+        rows = pl.ds(pl.multiple_of(block * 32, 32), 32)
+        for tile in range(12):
+            cols = slice(tile * 128, tile * 128 + 128)
+            value = wide16[0] * grads[0, rows, cols].reshape(2, 16, 128)
+            for k in range(1, 4):
+                value = value + wide16[k] * grads[k, rows, cols].reshape(2, 16, 128)
+            gcells[rows, cols] = value.reshape(32, 128).astype(BF16)
         return carry
 
-    lax.fori_loop(0, 4, in_plane, 0)
-    multiply(xlhs, 0, 4, 1, gz, 0)
-
-    def put_grad(layer, direction, tile, value):
-        base = direction * NODES + tile * 128
-        packed_in[rows_of(layer), base : base + 128] = (
-            (value * 0.125).reshape(LAYER, 128).astype(BF16)
-        )
-
-    packed_in = lhs
-    x_face = x_high | x_low
-    y_row = lax.broadcasted_iota(jnp.int32, (8, 8, 128), 0)
-    y_face = (y_high & (y_row < 7)) | (y_low & (y_row > 0))
-
-    def grad_layer(layer, z_low, z_high):
-        for tile in every:
-            value = load(gx, layer, tile)
-            value = jnp.where(x_face, 0.5, 1.0) * (value + x_neighbours(value))
-            put_grad(layer, 0, tile, value)
-            value = load(gy, layer, tile)
-            value = jnp.where(y_face, 0.5, 1.0) * (value + y_neighbours(value))
-            put_grad(layer, 1, tile, value)
-            value = load(gz, layer, tile)
-            if tile == 0:
-                if z_low is None:
-                    other, there = load(gz, layer - 1, 3), 1.0
-                    other = rotated(other, 64, 2)
-                else:
-                    other, there = z_low
-                mixed = value + (0.5 * there) * (other - value)
-                value = jnp.where(half_low, mixed, value)
-            if tile == 3:
-                if z_high is None:
-                    other, there = load(gz, layer + 1, 0), 1.0
-                    other = rotated(other, 64, 2)
-                else:
-                    other, there = z_high
-                mixed = value + (0.5 * there) * (other - value)
-                value = jnp.where(half_low, value, mixed)
-            put_grad(layer, 2, tile, value)
-
-    grad_layer(0, (fbuf[0].reshape(8, 8, 128), has_down), None)
-    over(1, 3, lambda layer: grad_layer(layer, None, None))
-    grad_layer(3, None, (fbuf[1].reshape(8, 8, 128), has_up))
+    lax.fori_loop(0, 8, combine_grads, 0)
 
     def pack(part, carry):
         cols = pl.ds(pl.multiple_of(part * 256, 256), 256)
         packed[:, cols] = jnp.dot(
-            gpack[...], packed_in[0:CELLS, cols], preferred_element_type=F32
+            gpack[...], gcells[:, cols], preferred_element_type=F32
         ).astype(BF16)
         return carry
 
@@ -595,18 +656,32 @@
             action(to_group(3 - grp, 0))
 
     each_send(lambda copy: copy.start())
-    recv[comp] = packed[pl.ds(pl.multiple_of(grp * LAYER, LAYER), LAYER), :]
-
-    def velocity_out(tile, carry):
-        cols = pl.ds(pl.multiple_of(tile * 128, 128), 128)
-        total = jnp.zeros((CELLS, 128), F32)
-        for part in split3(xs[:, cols]):
-            total = total + jnp.dot(ptr[...], part, preferred_element_type=F32)
-        out[:, cols] = total
-        return carry
+    own_slots = pl.ds(pl.multiple_of(grp * LAYER, LAYER), LAYER)
+    recv[comp] = packed[own_slots, :]
+
+    wide8 = [value.reshape(1, 8, 128) for value in coef]
 
     @pl.when(grp < 3)
     def _():
+        def solve_layer(layer):
+            for tile in every:
+                value = wide8[0] * load(v0, layer, tile)
+                for k in range(1, 4):
+                    value = value + wide8[k] * load(basis[k], layer, tile)
+                store(xs, layer - 4, tile, value)
+
+        over(4, 8, solve_layer)
+        for tile in every:
+            mirror_layers(xs[:, tile * 128 : tile * 128 + 128], tile, xstd, 0)
+
+        def velocity_out(tile, carry):
+            cols = pl.ds(pl.multiple_of(tile * 128, 128), 128)
+            total = jnp.zeros((CELLS, 128), F32)
+            for part in split3(xstd[:, cols]):
+                total = total + jnp.dot(ptr[...], part, preferred_element_type=F32)
+            out[:, cols] = total
+            return carry
+
         lax.fori_loop(0, 4, velocity_out, 0)
 
     each_send(lambda copy: copy.wait_send())
@@ -628,6 +703,21 @@
         return carry
 
     lax.fori_loop(0, 4, lambda_rows, 0)
+
+    odd_x, odd_y, odd_z = [
+        classes[own_slots, k * 128 : k * 128 + 128] > 0.5 for k in range(3)
+    ]
+    turned = []
+    for tile in every:
+        value = lam[:, tile * 128 : tile * 128 + 128]
+        rev_x, rev_y, rev_xy = reversals(value)
+        turned.append(
+            jnp.where(odd_x, jnp.where(odd_y, rev_xy, rev_x), jnp.where(odd_y, rev_y, value))
+        )
+    for tile in every:
+        lam[:, tile * 128 : tile * 128 + 128] = jnp.where(
+            odd_z, rotated(turned[3 - tile], 64, 1), turned[tile]
+        )
 
     base = grp * 8
     here = pl.ds(pl.multiple_of(dom * 8, 8), 8)
@@ -732,7 +822,7 @@
         scratch_shapes=[
             pltpu.VMEM(own, F32),
             pltpu.VMEM((8, NODES), F32),
-            pltpu.VMEM((384, 256), BF16),
+            pltpu.VMEM((512, 384), BF16),
             pltpu.VMEM((1, CELLS), jnp.int32),
             pltpu.VMEM((1, CELLS), jnp.int32),
             pltpu.VMEM((2, 3 * NODES, NODES), BF16),
@@ -751,12 +841,12 @@
             pltpu.VMEM(wide, F32),
             pltpu.VMEM(wide, F32),
             pltpu.VMEM(own, F32),
-            pltpu.VMEM((CELLS, 3 * NODES), BF16),
             pltpu.VMEM(own, F32),
-            pltpu.VMEM(own, F32),
+            pltpu.VMEM((4, CELLS, 3 * NODES), F32),
             pltpu.VMEM(own, F32),
             pltpu.VMEM((CELLS, CELLS), BF16),
-            pltpu.VMEM((2, LAYER, 128), F32),
+            pltpu.VMEM((CELLS, 384), F32),
+            pltpu.VMEM((CELLS, 3 * NODES), BF16),
             pltpu.VMEM((2, LAYER, 128), F32),
             pltpu.VMEM((2, LAYER, 128), F32),
             pltpu.VMEM((8, 128), F32),
@@ -765,8 +855,8 @@
             pltpu.VMEM((3, LAYER, 3 * NODES), BF16),
             pltpu.VMEM((LAYER, NODES), F32),
             pltpu.VMEM(own, F32),
-            dma((5,)), dma((7,)), dma, dma((2,)), dma((2,)), dma((4,)), dma((4,)), dma((2,)), dma((2,)),
-            dma, dma, dma((3,)), dma((3,)), dma((8,)), dma,
+            dma((6,)), dma((6,)), dma, dma((2,)), dma((2,)), dma((4,)), dma((4,)), dma((2,)),
+            dma((2,)), dma, dma, dma((3,)), dma((3,)), dma((8,)), dma,
         ],
         compiler_params=pltpu.CompilerParams(
             collective_id=0, has_side_effects=True, vmem_limit_bytes=60 * 1024 * 1024

time: 67.6 us -> 57.6 us (0.85)
  Pallas kernels: 65.6 us -> 55.5 us
    pallas_call x1, Pallas kernels: 65.6 us -> 55.5 us  [per_device(): pl.pallas_call(kernel, out_shape=jax.ShapeDtypeStruct(own, F32), in_specs...]
where the time goes in v2:
time: 57.6 us; the launch traced here: 57.4 us
  Pallas kernels  55.5 us (96%)
  local copies, waits for them, and re-layouts  1.87 us (3%)
    pallas_call x1, Pallas kernels, per_device(): pl.pallas_call(kernel, out_shape=jax.ShapeDtypeStruct(own, F32), in_specs...  55.5 us
    unnamed x1, local copies, waits for them, and re-layouts  1.87 us

profile of v2, /device:TPU:7, one launch (start us, length us, event | category | flops | bytes accessed | tf_op | source)
XLA Modules:
  0.0 57.4 jit_solution(4418227305956131980)
XLA Ops:
  0.0 55.5 %solve_and_analyse.1 = f32[256,512]{1,0:T(8,128)} custom-call(f32[3,256,512]{2,1,0:T(8,128)} %forcing.1, f32[1,256]{1,0:T(1,128)} %bitcast.4, f32[1,256]{1,0:T(1,128)} %bitcast.5, s32[1,256]{1,0:T(1,128)} %order_in.1, s32[1,256]{1,0:T(1,128)} %owner_in.1, f32[8,512]{1,0:T(8,128)} %constant.6.clone.lanes_in, bf16[512,384]{1,0:T(8,128)(2,1)} %constant.7.clone.flat_in, ...), custom_call_target="tpu_custom_call" | custom-call | tf_op jit(solution)/shard_map/solve_and_analyse/pallas_call | solution.py:817
  55.5 1.9 %copy.10 = f32[1,256,512]{2,1,0:T(8,128)} copy(f32[1,256,512]{2,1,0:T(8,128)} %bitcast.3) | data formatting | bytes 1048576

commit v3 on v2

--- a/solution.py
+++ b/solution.py
@@ -16,6 +16,8 @@
 CELLS = 256
 NODES = 512
 DOMS = 32
+HALF = 128
+CHUNK = 32
 BASIS_LOW = 0.3
 BASIS_HIGH = 2.0
 THETA = 0.5 * (BASIS_LOW + BASIS_HIGH)
@@ -76,7 +78,13 @@
     stiff = np.zeros((NODES, NODES))
     for matrix in directional:
         stiff = stiff + matrix.T @ (cube[:, None] * matrix)
-    mats = np.stack([np.stack(split_rows(m)) for m in (stiff, directional[2].T)])
+    flip = np.arange(NODES).reshape(NP, LAYER)[::-1][: NP // 2].reshape(-1)
+    mats = []
+    for matrix in (stiff, directional[2]):
+        near, far = matrix[:256, :256], matrix[:256, flip]
+        for block in (0.5 * (near + far), 0.5 * (near - far)):
+            mats.append(np.stack(split_rows(block.T)))
+    mats = np.stack(mats)
     flat = np.concatenate([directional[0].T[:128, :128], directional[1].T[:128, :128]], 1)
     high, low = split_rows(flat)
     flat = np.concatenate([high, high, low], 0)
@@ -84,6 +92,10 @@
     lanes[0] = cube
     lanes[1] = np.diag(stiff)
     lanes[2] = np.repeat(diff[0], LAYER)
+    order = [0, 1, 2, 3, 5, 4, 7, 6]
+    lanes = lanes.reshape(8, NP, LAYER)[:, order].reshape(8, NODES)
+    natural = cube.reshape(NP, LAYER).astype(np.float32).reshape(-1)
+    lanes[3] = natural
     back = eye[::-1]
     half = np.eye(2)
     mirror = np.concatenate(
@@ -94,7 +106,8 @@
         ],
         1,
     ).astype(ml_dtypes.bfloat16)
-    return mats, np.concatenate([np.concatenate([flat, np.zeros((384, 128), flat.dtype)], 1), mirror], 0), lanes
+    wide = np.concatenate([flat, np.zeros((384, 128), flat.dtype)], 1)
+    return mats, np.concatenate([wide, mirror, mirror], 0), lanes
 
 
 def rotated(value, shift, axis):
@@ -104,8 +117,8 @@
 def kernel(
     forcing, visc_in, mass_in, order_in, owner_in, lanes_in, flat_in, mats,
     out,
-    fsc, lanes, flat, order_sc, owner_sc, weights, par, parn, pone, ptr, visc, mass, raw, tmp,
-    inv, lhs, v0, v1, v2, v3, xs, xstd, grads, gz, gpack, classes, gcells, fsend, frecv, moments,
+    fsc, lanes, flat, order_sc, owner_sc, weights, par, parn, pone, ptr, parts, visc, mass, raw, tmp,
+    inv, lhs, v0, v1, v2, v3, xs, xstd, grads, gpack, classes, gcells, fsend, frecv, fghost, moments,
     red, packed, recv, lam, lamrecv,
     ssem, wsem, fsem, psend, precv, gsend, grecv, f3send, f3recv, rsend, rrecv, asend, arecv,
     osend, orecv,
@@ -146,11 +159,11 @@
     load_force = pltpu.make_async_copy(forcing.at[comp], fsc, fsem)
     load_force.start()
     load_mats = []
-    for which in range(2):
+    for which in range(4):
         for part, source in enumerate((0, 0, 1)):
             copy = pltpu.make_async_copy(
                 mats.at[which, source],
-                weights.at[which, part * NODES : (part + 1) * NODES],
+                weights.at[which, part * 256 : part * 256 + 256],
                 wsem.at[3 * which + part],
             )
             copy.start()
@@ -212,29 +225,25 @@
     def table(row, tile):
         return lanes[row : row + 1, tile * 128 : tile * 128 + 128].reshape(1, 1, 128)
 
-    def split3(value):
+    def split(value):
         high = value.astype(BF16)
-        rest = value - high.astype(F32)
-        middle = rest.astype(BF16)
-        low = (rest - middle.astype(F32)).astype(BF16)
-        return high, middle, low
-
-    def store_lhs(layer, tile, value):
-        value = value.reshape(LAYER, 128)
-        high = value.astype(BF16)
-        low = (value - high.astype(F32)).astype(BF16)
-        lhs[rows_of(layer), tile * 128 : tile * 128 + 128] = high
-        lhs[rows_of(layer), NODES + tile * 128 : NODES + tile * 128 + 128] = low
-        lhs[rows_of(layer), 2 * NODES + tile * 128 : 2 * NODES + tile * 128 + 128] = high
+        return high, (value - high.astype(F32)).astype(BF16)
+
+    def store_lhs(layer, pair, first, second):
+        for start, value in ((0, first + second), (768, first - second)):
+            start = start + pair * 128
+            high, low = split(value.reshape(LAYER, 128))
+            lhs[rows_of(layer), start : start + 128] = high
+            lhs[rows_of(layer), start + 256 : start + 384] = low
+            lhs[rows_of(layer), start + 512 : start + 640] = high
 
     def reversals(value):
-        total = None
-        for part in split3(value):
-            term = jnp.dot(part, flat[384:512, :], preferred_element_type=F32)
-            total = term if total is None else total + term
+        total = jnp.dot(
+            jnp.concatenate(split(value), 1), flat[384:640, :], preferred_element_type=F32
+        )
         return total[:, 0:128], total[:, 128:256], total[:, 256:384]
 
-    def mirror_layers(value, tile, target, base):
+    def mirror_layers(value, tile, target, base, back):
         flipped = reversals(value)
         for layer in range(4):
             rows = slice(layer * LAYER, layer * LAYER + LAYER)
@@ -246,10 +255,10 @@
             mixed = jnp.concatenate(
                 [(odd_y if k % 2 else even_y)[k : k + 1] for k in range(8)], 0
             )
-            if layer % 2:
-                store(target, base + layer, 3 - tile, rotated(mixed, 64, 2))
-            else:
-                store(target, base + layer, tile, mixed)
+            place = 3 - tile if layer % 2 else tile
+            if (place if back else tile) >= 2:
+                mixed = rotated(mixed, 64, 2)
+            store(target, base + layer, place, mixed)
 
     def over(low, high, body):
         lax.fori_loop(low, high, lambda layer, carry: (body(layer), carry)[1], 0)
@@ -268,15 +277,16 @@
             target[base : base + CELLS, :] = jnp.broadcast_to(col * scale, (CELLS, 128))
         return hit
 
-    pone[...] = jnp.where(par[2:3, :] == cell_sub, 1.0, 0.0).astype(BF16)
+    one_hot = jnp.where(par[2:3, :] == cell_sub, 1.0, 0.0).astype(BF16)
+    pone[:, 0:CELLS] = one_hot
+    pone[:, CELLS : 2 * CELLS] = one_hot
     load_force.wait()
+    high, low = split(fsc[...])
+    parts[0:CELLS, :] = high
+    parts[CELLS : 2 * CELLS, :] = low
+    fsc[...] = jnp.dot(pone[...], parts[...], preferred_element_type=F32) * lanes[3:4, :]
     for tile in every:
-        cols = slice(tile * 128, tile * 128 + 128)
-        total = None
-        for part in split3(fsc[:, cols]):
-            term = jnp.dot(pone[...], part, preferred_element_type=F32)
-            total = term if total is None else total + term
-        mirror_layers(total * lanes[0:1, cols], tile, raw, 4)
+        mirror_layers(fsc[:, tile * 128 : tile * 128 + 128], tile, raw, 4, False)
 
     pl.semaphore_wait(barrier, DOMS - 1 + 3)
 
@@ -315,7 +325,9 @@
     order_col = jnp.sum(
         jnp.where(cell_sub == cell_lane, par[2:3, :], 0.0), axis=1, keepdims=True
     )
-    ptr[...] = jnp.where(order_col == cell_lane, 1.0, 0.0).astype(BF16)
+    one_hot = jnp.where(order_col == cell_lane, 1.0, 0.0).astype(BF16)
+    ptr[:, 0:CELLS] = one_hot
+    ptr[:, CELLS : 2 * CELLS] = one_hot
     owner_row = owner_sc[...].astype(F32)
     owner_col = jnp.sum(
         jnp.where(cell_sub == cell_lane, owner_row, 0.0), axis=1, keepdims=True
@@ -324,7 +336,7 @@
     rank_row = jnp.sum(jnp.where(same, 1.0, 0.0), axis=0, keepdims=True)
     dest_row = jnp.where(owner_row >= 0.0, owner_row * 8.0 + rank_row, -1.0)
     slot_of = jnp.where(dest_row == cell_sub, 1.0, 0.0).astype(BF16)
-    gpack[...] = jnp.dot(slot_of, ptr[...], preferred_element_type=F32).astype(BF16)
+    gpack[...] = jnp.dot(slot_of, one_hot, preferred_element_type=F32).astype(BF16)
     cell_id = lax.broadcasted_iota(jnp.int32, (CELLS, 128), 0)
     for k, width in enumerate((1, 8, 64)):
         parity = lax.rem(cell_id // width, 2).astype(F32).astype(BF16)
@@ -344,9 +356,7 @@
     def face_sum(ref, layer, tile):
         value = load(ref, layer, tile)
         other = load(ref, partners(layer)[tile], tile)
-        if tile == 0:
-            return value + jnp.where(low_half, other, 0.0)
-        return value + jnp.where(low_half, 0.0, other)
+        return value + jnp.where(low_half, other, 0.0)
 
     def put_inverse(layer, tile, diag):
         store(inv, layer, tile, jnp.where(diag > 0.0, (2.0 / DELTA) / diag, 0.0))
@@ -371,12 +381,16 @@
 
     over(1, 11, diagonal_faces)
 
-    def put_first(layer, tile, force):
-        value = force * load(inv, layer, tile) * (0.5 * DELTA)
-        store(v0, layer, tile, value)
-        store_lhs(layer, tile, value)
+    def put_first(layer, pair, forces):
+        values = []
+        for tile, force in zip((pair, 3 - pair), forces):
+            value = force * load(inv, layer, tile) * (0.5 * DELTA)
+            store(v0, layer, tile, value)
+            values.append(value)
+        store_lhs(layer, pair, *values)
 
     def assemble(layer, tiles, scale):
+        sums = []
         for tile in tiles:
             force = load(raw, layer, tile)
             if scale is not None:
@@ -385,7 +399,9 @@
             if tile in (0, 3):
                 store(tmp, layer, tile, force)
             else:
-                put_first(layer, tile, force)
+                sums.append(force)
+        if sums:
+            put_first(layer, 1, sums)
 
     over(4, 8, lambda layer: assemble(layer, every, None))
     for copy in load_mats:
@@ -398,63 +414,71 @@
     assemble(11, (3,), has_up)
 
     def first_faces(layer):
-        for tile in (0, 3):
-            put_first(layer, tile, face_sum(tmp, layer, tile))
+        put_first(layer, 0, [face_sum(tmp, layer, tile) for tile in (0, 3)])
 
     over(1, 11, first_faces)
 
-    def multiply(low, high, which, target, target_low):
-        def body(half, carry):
-            cols = pl.ds(pl.multiple_of(half * 256, 256), 256)
-            target[target_low * LAYER : (target_low + high - low) * LAYER, cols] = jnp.dot(
-                lhs[low * LAYER : high * LAYER, :],
-                weights[which, :, cols],
+    def multiply(low, high, which, target, first=0):
+        for part in range(2):
+            target[:, first + part * 256 : first + part * 256 + 256] = jnp.dot(
+                lhs[low * LAYER : high * LAYER, part * 768 : part * 768 + 768],
+                weights[2 * which + part],
                 preferred_element_type=F32,
             )
-            return carry
-
-        lax.fori_loop(0, 2, body, 0)
-
-    def advance(step, layer, tile, total):
-        value = total * load(inv, layer, tile)
-        current = load(basis[step], layer, tile)
-        if step == 0:
-            value = 0.5 * value - (THETA / DELTA) * current
-        else:
-            value = value - (2.0 * THETA / DELTA) * current - load(basis[step - 1], layer, tile)
-        store(basis[step + 1], layer, tile, value)
-        store_lhs(layer, tile, value)
+
+    def advance(step, layer, pair, totals):
+        values = []
+        for tile, total in zip((pair, 3 - pair), totals):
+            value = total * load(inv, layer, tile)
+            current = load(basis[step], layer, tile)
+            if step == 0:
+                value = 0.5 * value - (THETA / DELTA) * current
+            else:
+                value = value - (2.0 * THETA / DELTA) * current
+                value = value - load(basis[step - 1], layer, tile)
+            store(basis[step + 1], layer, tile, value)
+            values.append(value)
+        store_lhs(layer, pair, *values)
 
     def apply(step, layer, tiles, sums, going):
         coef_v = column(visc, layer)
         coef_m = column(mass, layer)
-        for tile in tiles:
-            value = load(basis[step], layer, tile)
-            weighted = coef_m * table(0, tile)
-            image = coef_v * load(tmp, layer, tile) + weighted * value
-            if sums is not None:
-                diag = coef_v * table(1, tile) + weighted
-                sums = (
-                    sums[0] + jnp.sum(value * image, axis=0),
-                    sums[1] + jnp.sum(value * value * diag, axis=0),
-                )
-            if going:
-                image = xy_sum(image)
-                if tile in (0, 3):
-                    store(tmp, layer, tile, image)
-                else:
-                    advance(step, layer, tile, image)
+        for pair in (1, 0):
+            if pair not in tiles and 3 - pair not in tiles:
+                continue
+            even = load(tmp, layer, pair)
+            uneven = load(tmp, layer, 2 + pair)
+            images = []
+            for tile, product in ((pair, even + uneven), (3 - pair, even - uneven)):
+                if tile not in tiles:
+                    continue
+                value = load(basis[step], layer, tile)
+                weighted = coef_m * table(0, tile)
+                image = coef_v * product + weighted * value
+                if sums is not None:
+                    diag = coef_v * table(1, tile) + weighted
+                    sums = (
+                        sums[0] + jnp.sum(value * image, axis=0),
+                        sums[1] + jnp.sum(value * value * diag, axis=0),
+                    )
+                if going:
+                    image = xy_sum(image)
+                    if pair == 0:
+                        store(tmp, layer, tile, image)
+                    else:
+                        images.append(image)
+            if images:
+                advance(step, layer, 1, images)
         return sums
 
     def faces(step, layer):
-        for tile in (0, 3):
-            advance(step, layer, tile, face_sum(tmp, layer, tile))
+        advance(step, layer, 0, [face_sum(tmp, layer, tile) for tile in (0, 3)])
 
     blank_sums = (jnp.zeros((8, 128), F32), jnp.zeros((8, 128), F32))
     for step in range(ITERS):
         low, high = 1 + step, 11 - step
         going = step + 1 < ITERS
-        multiply(low, high, 0, tmp, low)
+        multiply(low, high, 0, tmp.at[low * LAYER : high * LAYER])
         if going:
             inward = 0 if low % 2 else 3
             apply(step, low, (inward,), None, True)
@@ -492,75 +516,50 @@
     for copy in face_copies:
         copy.start()
 
-    x_sign = jnp.where(odd, -1.0, 1.0).reshape(1, 8, 128)
-    x_scale = jnp.where(take_up | take_down, 0.5, 1.0).reshape(1, 8, 128) * x_sign
-    y_half = jnp.where((node_j == 7) | (node_j == 0), 0.5, 1.0).reshape(1, 8, 128)
-    y_end = jnp.where(node_j == 7, 0.5, 1.0).reshape(1, 8, 128)
-    y_scale = jnp.concatenate(
-        [y_end, -y_half, y_half, -y_half, y_half, -y_half, y_half, -y_end], 0
-    )
-
-    def refill(ref):
-        def body(layer):
-            for tile in every:
-                store_lhs(layer, tile, load(ref, layer, tile))
-
-        over(4, 8, body)
-
-    for index in range(ITERS):
-        vec = basis[index]
-        if index < ITERS - 1:
-            refill_needed = True
-        else:
-            refill_needed = True
-        if refill_needed:
-            refill(vec)
-        own_rows = slice(4 * LAYER, 8 * LAYER)
-
-        def in_plane(tile, carry, index=index):
-            start = pl.multiple_of(tile * 128, 128)
-            left = jnp.concatenate(
-                [lhs[own_rows, pl.ds(part * NODES + start, 128)] for part in range(3)], 1
+    own_rows = slice(4 * LAYER, 8 * LAYER)
+    for index in (3, 0, 1, 2):
+        if index < 3:
+            over(
+                4,
+                8,
+                lambda layer: [
+                    store_lhs(
+                        layer,
+                        pair,
+                        load(basis[index], layer, pair),
+                        load(basis[index], layer, 3 - pair),
+                    )
+                    for pair in (0, 1)
+                ],
             )
-            both = jnp.dot(left, flat[0:384, 0:256], preferred_element_type=F32)
-            for layer in range(4):
-                rows = slice(layer * LAYER, layer * LAYER + LAYER)
-                value = both[rows, 0:128].reshape(8, 8, 128)
-                value = x_scale * (value - x_others(value))
-                grads[index, rows, pl.ds(start, 128)] = value.reshape(LAYER, 128)
-                value = both[rows, 128:256].reshape(8, 8, 128)
-                value = y_scale * (value - y_others(value))
-                grads[index, rows, pl.ds(NODES + start, 128)] = value.reshape(LAYER, 128)
-            return carry
-
-        lax.fori_loop(0, 4, in_plane, 0)
-        multiply(4, 8, 1, gz, 0)
-        if index == ITERS - 1:
-            for copy in face_copies:
-                copy.wait()
-        for layer in range(4):
-            sign = -1.0 if layer % 2 else 1.0
-            for tile in every:
-                value = load(gz, layer, tile) * sign
-                if tile == 0:
-                    if layer in (0, 3):
-                        side = 0 if layer == 0 else 1
-                        if index == ITERS - 1:
-                            other = frecv[side].reshape(8, 8, 128)
-                        else:
-                            other = end_face(vec, 3 if side == 0 else 8)
-                        there = 0.5 * (has_down if side == 0 else has_up)
-                    else:
-                        other = load(gz, 3 - layer, 0) * -sign
-                        there = 0.5
-                    value = value + jnp.where(low_half, there * (other - value), 0.0)
-                if tile == 3:
-                    other = load(gz, layer ^ 1, 3) * -sign
-                    value = value + jnp.where(low_half, 0.0, 0.5 * (other - value))
-                base = 2 * NODES + tile * 128
-                grads[index, layer * LAYER : layer * LAYER + LAYER, base : base + 128] = (
-                    value.reshape(LAYER, 128)
+
+        left = jnp.concatenate(
+            [
+                jnp.concatenate(
+                    [
+                        lhs[own_rows, start + part * 256 : start + part * 256 + 128]
+                        for part in range(3)
+                    ],
+                    1,
                 )
+                for start in (0, 128, 768, 896)
+            ],
+            0,
+        )
+        both = jnp.dot(left, flat[0:384, 0:256], preferred_element_type=F32)
+        for part in range(4):
+            rows = slice(part * CELLS, part * CELLS + CELLS)
+            grads[index, :, part * 128 : part * 128 + 128] = both[rows, 0:128]
+            grads[index, :, NODES + part * 128 : NODES + part * 128 + 128] = both[rows, 128:256]
+        multiply(4, 8, 1, grads.at[index], 2 * NODES)
+        if index < 3:
+            fghost[index, 0] = end_face(basis[index], 3).reshape(LAYER, 128)
+            fghost[index, 1] = end_face(basis[index], 8).reshape(LAYER, 128)
+
+    for copy in face_copies:
+        copy.wait()
+    for side in range(2):
+        fghost[3, side] = frecv[side]
 
     whole = remote(red.at[1:DOMS], red.at[1:DOMS], rsend, rrecv, (grp, up))
     whole.wait_send()
@@ -613,51 +612,98 @@
             value = value - gram[k][j] * coef[j]
         coef[k] = value * pivots[k]
 
-    wide16 = [
-        jnp.concatenate([value * (1.0 / NP)] * 2, 0).reshape(1, 16, 128) for value in coef
+    coef8 = [(value * (1.0 / NP)).reshape(1, 8, 128) for value in coef]
+    coef16 = [0.5 * value for value in coef8]
+    x_sign = jnp.where(odd, -1.0, 1.0).reshape(1, 8, 128)
+    x_scale = jnp.where(take_up | take_down, 0.5, 1.0).reshape(1, 8, 128) * x_sign
+    y_half = jnp.where((node_j == 7) | (node_j == 0), 0.5, 1.0).reshape(1, 8, 128)
+    y_end = jnp.where(node_j == 7, 0.5, 1.0).reshape(1, 8, 128)
+    y_scale = jnp.concatenate(
+        [y_end, -y_half, y_half, -y_half, y_half, -y_half, y_half, -y_end], 0
+    )
+
+    def combined(layer, direction, pair):
+        parts_of = []
+        scale = coef8 if direction == 2 else coef16
+        for start in (0, 256):
+            start = start + direction * NODES + pair * 128
+            value = None
+            for k in range(4):
+                term = scale[k] * grads[k, rows_of(layer), start : start + 128].reshape(8, 8, 128)
+                value = term if value is None else value + term
+            parts_of.append(value)
+        even, uneven = parts_of
+        if direction == 2:
+            return even + uneven, uneven - even
+        return even + uneven, even - uneven
+
+    def put_grad(layer, direction, tile, value):
+        start = direction * NODES + tile * 128
+        gcells[rows_of(layer), start : start + 128] = value.reshape(LAYER, 128).astype(BF16)
+
+    def flat_grads(layer):
+        z_sign = (1 - 2 * lax.rem(layer, 2)).astype(F32)
+        for pair in (0, 1):
+            for tile, value in zip((pair, 3 - pair), combined(layer, 0, pair)):
+                put_grad(layer, 0, tile, x_scale * (value - x_others(value)))
+            for tile, value in zip((pair, 3 - pair), combined(layer, 1, pair)):
+                put_grad(layer, 1, tile, y_scale * (value - y_others(value)))
+        for tile, value in zip((1, 2), combined(layer, 2, 1)):
+            put_grad(layer, 2, tile, z_sign * value)
+        for tile, value in zip((0, 3), combined(layer, 2, 0)):
+            store(xstd, layer, tile, z_sign * value)
+
+    over(0, 4, flat_grads)
+
+    def mean_face(layer, tile, other, there):
+        value = load(xstd, layer, tile)
+        put_grad(layer, 2, tile, value + jnp.where(low_half, there * (other - value), 0.0))
+
+    for layer in range(4):
+        mean_face(layer, 3, load(xstd, layer ^ 1, 3), 0.5)
+        if layer in (1, 2):
+            mean_face(layer, 0, load(xstd, 3 - layer, 0), 0.5)
+        else:
+            side = 0 if layer == 0 else 1
+            other = None
+            for k in range(4):
+                term = coef8[k] * fghost[k, side].reshape(8, 8, 128)
+                other = term if other is None else other + term
+            mean_face(layer, 0, other, 0.5 * (has_up if side else has_down))
+
+    target = 1 - lax.rem(grp, 2)
+    source = lax.div(grp, 2)
+    send_slots = pl.ds(pl.multiple_of(target * HALF, HALF), HALF)
+    own_slots = pl.ds(pl.multiple_of((1 - target) * HALF, HALF), HALF)
+
+    def pack(slots, into):
+        def body(part, carry):
+            cols = pl.ds(pl.multiple_of(part * 512, 512), 512)
+            into[:, cols] = jnp.dot(
+                gpack[slots, :], gcells[:, cols], preferred_element_type=F32
+            ).astype(BF16)
+            return carry
+
+        lax.fori_loop(0, 3, body, 0)
+
+    pack(send_slots, packed)
+
+    def chunk_rows(chunk):
+        return slice(chunk * CHUNK, chunk * CHUNK + CHUNK)
+
+    group_copies = [
+        remote(
+            packed.at[chunk_rows(chunk)], recv.at[comp, chunk_rows(chunk)],
+            asend.at[chunk], arecv.at[source, chunk], (target, dom),
+        )
+        for chunk in range(HALF // CHUNK)
     ]
-
-    def combine_grads(block, carry):
-        rows = pl.ds(pl.multiple_of(block * 32, 32), 32)
-        for tile in range(12):
-            cols = slice(tile * 128, tile * 128 + 128)
-            value = wide16[0] * grads[0, rows, cols].reshape(2, 16, 128)
-            for k in range(1, 4):
-                value = value + wide16[k] * grads[k, rows, cols].reshape(2, 16, 128)
-            gcells[rows, cols] = value.reshape(32, 128).astype(BF16)
-        return carry
-
-    lax.fori_loop(0, 8, combine_grads, 0)
-
-    def pack(part, carry):
-        cols = pl.ds(pl.multiple_of(part * 256, 256), 256)
-        packed[:, cols] = jnp.dot(
-            gpack[...], gcells[:, cols], preferred_element_type=F32
-        ).astype(BF16)
-        return carry
-
-    lax.fori_loop(0, 6, pack, 0)
-
-    def to_group(target, slot):
-        start = pl.multiple_of(target * LAYER, LAYER)
-        return remote(
-            packed.at[pl.ds(start, LAYER)], recv.at[comp],
-            asend.at[slot], arecv.at[comp], (target, dom),
-        )
-
-    def each_send(action):
-        @pl.when(grp < 2)
-        def _():
-            for step in range(1, 4):
-                action(to_group(lax.rem(grp + step, 4), step - 1))
-
-        @pl.when(grp >= 2)
-        def _():
-            action(to_group(3 - grp, 0))
-
-    each_send(lambda copy: copy.start())
-    own_slots = pl.ds(pl.multiple_of(grp * LAYER, LAYER), LAYER)
-    recv[comp] = packed[own_slots, :]
+    for copy in group_copies:
+        copy.start()
+
+    @pl.when(grp < 2)
+    def _():
+        pack(own_slots, recv.at[comp])
 
     wide8 = [value.reshape(1, 8, 128) for value in coef]
 
@@ -672,22 +718,11 @@
 
         over(4, 8, solve_layer)
         for tile in every:
-            mirror_layers(xs[:, tile * 128 : tile * 128 + 128], tile, xstd, 0)
-
-        def velocity_out(tile, carry):
-            cols = pl.ds(pl.multiple_of(tile * 128, 128), 128)
-            total = jnp.zeros((CELLS, 128), F32)
-            for part in split3(xstd[:, cols]):
-                total = total + jnp.dot(ptr[...], part, preferred_element_type=F32)
-            out[:, cols] = total
-            return carry
-
-        lax.fori_loop(0, 4, velocity_out, 0)
-
-    each_send(lambda copy: copy.wait_send())
-    for step in (1, 2):
-        other = lax.rem(comp + step, 3)
-        remote(recv.at[other], recv.at[other], asend.at[0], arecv.at[other], (grp, up)).wait_recv()
+            mirror_layers(xs[:, tile * 128 : tile * 128 + 128], tile, xstd, 0, True)
+        high, low = split(xstd[...])
+        parts[0:CELLS, :] = high
+        parts[CELLS : 2 * CELLS, :] = low
+        out[...] = jnp.dot(ptr[...], parts[...], preferred_element_type=F32)
 
     def lambda_rows(block, carry):
         rows = pl.ds(pl.multiple_of(block * 16, 16), 16)
@@ -702,62 +737,60 @@
             lam[rows, part * 256 : part * 256 + 256] = lambda_two(jac)
         return carry
 
-    lax.fori_loop(0, 4, lambda_rows, 0)
-
-    odd_x, odd_y, odd_z = [
-        classes[own_slots, k * 128 : k * 128 + 128] > 0.5 for k in range(3)
-    ]
-    turned = []
-    for tile in every:
-        value = lam[:, tile * 128 : tile * 128 + 128]
-        rev_x, rev_y, rev_xy = reversals(value)
-        turned.append(
-            jnp.where(odd_x, jnp.where(odd_y, rev_xy, rev_x), jnp.where(odd_y, rev_y, value))
-        )
-    for tile in every:
-        lam[:, tile * 128 : tile * 128 + 128] = jnp.where(
-            odd_z, rotated(turned[3 - tile], 64, 1), turned[tile]
-        )
-
-    base = grp * 8
+    def natural_order(chunk):
+        rows = chunk_rows(chunk)
+        start = pl.multiple_of((1 - target) * HALF, HALF) + chunk * CHUNK
+        slots = pl.ds(pl.multiple_of(start, CHUNK), CHUNK)
+        odd_x, odd_y, odd_z = [
+            classes[slots, k * 128 : k * 128 + 128] > 0.5 for k in range(3)
+        ]
+        values = [lam[rows, tile * 128 : tile * 128 + 128] for tile in every]
+        flipped = reversals(jnp.concatenate(values, 0))
+        turned = []
+        for tile in every:
+            rev_x, rev_y, rev_xy = [part[chunk_rows(tile)] for part in flipped]
+            turned.append(
+                jnp.where(
+                    odd_x,
+                    jnp.where(odd_y, rev_xy, rev_x),
+                    jnp.where(odd_y, rev_y, values[tile]),
+                )
+            )
+        for tile in every:
+            value = jnp.where(odd_z, turned[3 - tile], turned[tile])
+            if tile >= 2:
+                value = rotated(value, 64, 1)
+            lam[rows, tile * 128 : tile * 128 + 128] = value
+
     here = pl.ds(pl.multiple_of(dom * 8, 8), 8)
 
     def to_owner(k):
         return remote(
-            lam.at[8 * k : 8 * k + 8], lamrecv.at[here], osend.at[k], orecv, (3, base + k)
-        )
-
-    def each_owner(action):
-        for k in range(8):
-            own = (grp == 3) & (base + k == dom)
-
-            @pl.when(jnp.logical_not(own))
-            def _():
-                action(to_owner(k))
-
-    each_owner(lambda copy: copy.start())
-    for k in range(8):
-
-        @pl.when((grp == 3) & (base + k == dom))
-        def _():
-            lamrecv[here, :] = lam[8 * k : 8 * k + 8, :]
-
-    each_owner(lambda copy: copy.wait_send())
-
-    def wait_rows(count):
-        piece = lamrecv.at[0 : 8 * count]
-        remote(piece, piece, osend.at[0], orecv, (grp, up)).wait_recv()
-
-    @pl.when((grp == 3) & (dom >= 24))
+            lam.at[8 * k : 8 * k + 8], lamrecv.at[here], osend.at[k], orecv,
+            (3, (1 - target) * (HALF // 8) + k),
+        )
+
+    @pl.when(grp < 2)
     def _():
-        wait_rows(31)
-
-    @pl.when((grp == 3) & (dom < 24))
-    def _():
-        wait_rows(32)
+        for chunk in range(HALF // CHUNK):
+            for which, other in ((0, 1 - grp), (1, 2)):
+                piece = recv.at[other, chunk_rows(chunk)]
+                remote(
+                    piece, piece, asend.at[chunk], arecv.at[which, chunk], (target, dom)
+                ).wait_recv()
+            lax.fori_loop(chunk * CHUNK // 16, (chunk + 1) * CHUNK // 16, lambda_rows, 0)
+            natural_order(chunk)
+            for k in range(chunk * CHUNK // 8, (chunk + 1) * CHUNK // 8):
+                to_owner(k).start()
+        for k in range(HALF // 8):
+            to_owner(k).wait_send()
+
+    for copy in group_copies:
+        copy.wait_send()
 
     @pl.when(grp == 3)
     def _():
+        remote(lamrecv, lamrecv, osend.at[0], orecv, (target, dom)).wait_recv()
         out[...] = lamrecv[...]
 
 
@@ -816,20 +849,21 @@
     dma = pltpu.SemaphoreType.DMA
     result = pl.pallas_call(
         kernel,
-        out_shape=jax.ShapeDtypeStruct(own, F32),
+        out_shape=pltpu.VMEM(own, F32),
         in_specs=[hbm] * 8,
         out_specs=vmem,
         scratch_shapes=[
             pltpu.VMEM(own, F32),
             pltpu.VMEM((8, NODES), F32),
-            pltpu.VMEM((512, 384), BF16),
+            pltpu.VMEM((640, 384), BF16),
             pltpu.VMEM((1, CELLS), jnp.int32),
             pltpu.VMEM((1, CELLS), jnp.int32),
-            pltpu.VMEM((2, 3 * NODES, NODES), BF16),
+            pltpu.VMEM((4, 768, 256), BF16),
             pltpu.VMEM((8, CELLS), F32),
             pltpu.VMEM((2, 8, CELLS), F32),
-            pltpu.VMEM((CELLS, CELLS), BF16),
-            pltpu.VMEM((CELLS, CELLS), BF16),
+            pltpu.VMEM((CELLS, 2 * CELLS), BF16),
+            pltpu.VMEM((CELLS, 2 * CELLS), BF16),
+            pltpu.VMEM((2 * CELLS, NODES), BF16),
             pltpu.VMEM((12 * LAYER, 128), F32),
             pltpu.VMEM((12 * LAYER, 128), F32),
             pltpu.VMEM(wide, F32),
@@ -843,20 +877,20 @@
             pltpu.VMEM(own, F32),
             pltpu.VMEM(own, F32),
             pltpu.VMEM((4, CELLS, 3 * NODES), F32),
-            pltpu.VMEM(own, F32),
             pltpu.VMEM((CELLS, CELLS), BF16),
             pltpu.VMEM((CELLS, 384), F32),
             pltpu.VMEM((CELLS, 3 * NODES), BF16),
             pltpu.VMEM((2, LAYER, 128), F32),
             pltpu.VMEM((2, LAYER, 128), F32),
+            pltpu.VMEM((4, 2, LAYER, 128), F32),
             pltpu.VMEM((8, 128), F32),
             pltpu.VMEM((DOMS, 8, 128), F32),
-            pltpu.VMEM((CELLS, 3 * NODES), BF16),
-            pltpu.VMEM((3, LAYER, 3 * NODES), BF16),
-            pltpu.VMEM((LAYER, NODES), F32),
+            pltpu.VMEM((HALF, 3 * NODES), BF16),
+            pltpu.VMEM((3, HALF, 3 * NODES), BF16),
+            pltpu.VMEM((HALF, NODES), F32),
             pltpu.VMEM(own, F32),
-            dma((6,)), dma((6,)), dma, dma((2,)), dma((2,)), dma((4,)), dma((4,)), dma((2,)),
-            dma((2,)), dma, dma, dma((3,)), dma((3,)), dma((8,)), dma,
+            dma((6,)), dma((12,)), dma, dma((2,)), dma((2,)), dma((4,)), dma((4,)), dma((2,)),
+            dma((2,)), dma, dma, dma((HALF // CHUNK,)), dma((2, HALF // CHUNK)), dma((HALF // 8,)), dma,
         ],
         compiler_params=pltpu.CompilerParams(
             collective_id=0, has_side_effects=True, vmem_limit_bytes=60 * 1024 * 1024

time: 57.6 us -> 50.9 us (0.88)
  the two profiles are of different devices: /device:TPU:7 before, /device:TPU:15 now
where the time goes in v3:
time: 50.9 us; the launch traced here: 50.8 us
  Pallas kernels  50 us (98%)
  local copies, waits for them, and re-layouts  0.8 us (2%)
    pallas_call x1, Pallas kernels, per_device(): pl.pallas_call(kernel, out_shape=pltpu.VMEM(own, F32), in_specs=[hbm] * 8...  50 us

profile of v3, /device:TPU:15, one launch (start us, length us, event | category | flops | bytes accessed | tf_op | source)
XLA Modules:
  0.0 50.8 jit_solution(6515045507288789107)
XLA Ops:
  0.0 50.0 %solve_and_analyse.1 = f32[256,512]{1,0:T(8,128)S(1)} custom-call(f32[3,256,512]{2,1,0:T(8,128)} %forcing.1, f32[1,256]{1,0:T(1,128)} %bitcast.4, f32[1,256]{1,0:T(1,128)} %bitcast.5, s32[1,256]{1,0:T(1,128)} %order_in.1, s32[1,256]{1,0:T(1,128)} %owner_in.1, f32[8,512]{1,0:T(8,128)} %constant.6.clone.lanes_in, bf16[640,384]{1,0:T(8,128)(2,1)} %constant.7.clone.flat_in, ...), custom_call_target="tpu_custom_call" | custom-call | tf_op jit(solution)/shard_map/solve_and_analyse/pallas_call | solution.py:850
  50.0 0.8 %copy.10 = f32[1,256,512]{2,1,0:T(8,128)} copy(f32[1,256,512]{2,1,0:T(8,128)S(1)} %bitcast.3) | data formatting | bytes 1048576

commit v4 on v3

--- a/solution.py
+++ b/solution.py
@@ -16,8 +16,8 @@
 CELLS = 256
 NODES = 512
 DOMS = 32
-HALF = 128
 CHUNK = 32
+SHARE = 96
 BASIS_LOW = 0.3
 BASIS_HIGH = 2.0
 THETA = 0.5 * (BASIS_LOW + BASIS_HIGH)
@@ -334,7 +334,11 @@
     )
     same = (owner_col == owner_row) & (cell_sub < cell_lane)
     rank_row = jnp.sum(jnp.where(same, 1.0, 0.0), axis=0, keepdims=True)
-    dest_row = jnp.where(owner_row >= 0.0, owner_row * 8.0 + rank_row, -1.0)
+    owner_int = owner_sc[...]
+    place = owner_int >> 3
+    piece_row = ((((owner_int >> 1) - place) & 3) << 1) + (owner_int & 1)
+    first_row = (piece_row * 4 + place).astype(F32)
+    dest_row = jnp.where(owner_row >= 0.0, first_row * 8.0 + rank_row, -1.0)
     slot_of = jnp.where(dest_row == cell_sub, 1.0, 0.0).astype(BF16)
     gpack[...] = jnp.dot(slot_of, one_hot, preferred_element_type=F32).astype(BF16)
     cell_id = lax.broadcasted_iota(jnp.int32, (CELLS, 128), 0)
@@ -673,10 +677,12 @@
 
     target = 1 - lax.rem(grp, 2)
     source = lax.div(grp, 2)
-    send_slots = pl.ds(pl.multiple_of(target * HALF, HALF), HALF)
-    own_slots = pl.ds(pl.multiple_of((1 - target) * HALF, HALF), HALF)
-
-    def pack(slots, into):
+    own_first = jnp.where(grp == 3, 2, lax.rem(grp, 2)) * SHARE
+    own_count = jnp.where(grp == 3, 2, 3)
+
+    def pack(first, count, into):
+        slots = pl.ds(pl.multiple_of(first, CHUNK), count)
+
         def body(part, carry):
             cols = pl.ds(pl.multiple_of(part * 512, 512), 512)
             into[:, cols] = jnp.dot(
@@ -686,24 +692,35 @@
 
         lax.fori_loop(0, 3, body, 0)
 
-    pack(send_slots, packed)
-
     def chunk_rows(chunk):
-        return slice(chunk * CHUNK, chunk * CHUNK + CHUNK)
-
-    group_copies = [
-        remote(
-            packed.at[chunk_rows(chunk)], recv.at[comp, chunk_rows(chunk)],
-            asend.at[chunk], arecv.at[source, chunk], (target, dom),
-        )
-        for chunk in range(HALF // CHUNK)
-    ]
-    for copy in group_copies:
+        return pl.ds(pl.multiple_of(chunk * CHUNK, CHUNK), CHUNK)
+
+    def turn(step, count):
+        return lax.rem(dom + step, count)
+
+    def piece_copy(start, chunk, slot, device, which):
+        return remote(
+            packed.at[chunk_rows(start + chunk)], recv.at[comp, chunk_rows(chunk)],
+            asend.at[slot], arecv.at[which, chunk], (device, dom),
+        )
+
+    pack(target * SHARE, SHARE, packed.at[0:SHARE])
+
+    first_copies = [piece_copy(0, turn(k, 3), k, target, source) for k in range(3)]
+    second_copies = [piece_copy(3, turn(k, 2), 3 + k, 3, grp) for k in range(2)]
+    for copy in first_copies:
         copy.start()
 
     @pl.when(grp < 2)
     def _():
-        pack(own_slots, recv.at[comp])
+        pack(2 * SHARE, CELLS - 2 * SHARE, packed.at[SHARE : SHARE + CELLS - 2 * SHARE])
+        for copy in second_copies:
+            copy.start()
+        pack(own_first, SHARE, recv.at[comp])
+
+    @pl.when(grp == 3)
+    def _():
+        pack(own_first, CELLS - 2 * SHARE, recv.at[comp, 0 : CELLS - 2 * SHARE])
 
     wide8 = [value.reshape(1, 8, 128) for value in coef]
 
@@ -739,8 +756,7 @@
 
     def natural_order(chunk):
         rows = chunk_rows(chunk)
-        start = pl.multiple_of((1 - target) * HALF, HALF) + chunk * CHUNK
-        slots = pl.ds(pl.multiple_of(start, CHUNK), CHUNK)
+        slots = pl.ds(pl.multiple_of(own_first + chunk * CHUNK, CHUNK), CHUNK)
         odd_x, odd_y, odd_z = [
             classes[slots, k * 128 : k * 128 + 128] > 0.5 for k in range(3)
         ]
@@ -748,7 +764,9 @@
         flipped = reversals(jnp.concatenate(values, 0))
         turned = []
         for tile in every:
-            rev_x, rev_y, rev_xy = [part[chunk_rows(tile)] for part in flipped]
+            rev_x, rev_y, rev_xy = [
+                part[tile * CHUNK : tile * CHUNK + CHUNK] for part in flipped
+            ]
             turned.append(
                 jnp.where(
                     odd_x,
@@ -764,33 +782,78 @@
 
     here = pl.ds(pl.multiple_of(dom * 8, 8), 8)
 
-    def to_owner(k):
-        return remote(
-            lam.at[8 * k : 8 * k + 8], lamrecv.at[here], osend.at[k], orecv,
-            (3, (1 - target) * (HALF // 8) + k),
-        )
+    def each_owner(chunk, action, local):
+        piece = lax.div(own_first, CHUNK) + chunk
+        for place in range(4):
+            owner = place * 8 + lax.rem(place + lax.div(piece, 2), 4) * 2 + lax.rem(piece, 2)
+            rows = pl.ds(pl.multiple_of(chunk * CHUNK + place * 8, 8), 8)
+            own = (grp == 3) & (owner == dom)
+
+            @pl.when(jnp.logical_not(own))
+            def _():
+                action(
+                    remote(
+                        lam.at[rows], lamrecv.at[here], osend.at[chunk * 4 + place], orecv,
+                        (3, owner),
+                    )
+                )
+
+            if local:
+
+                @pl.when(own)
+                def _():
+                    lamrecv[here, :] = lam[rows, :]
+
+    def analyse(chunk):
+        others = (jnp.where(grp == 0, 1, 0), jnp.where(grp == 3, 1, 2))
+        for which in range(2):
+            piece = recv.at[others[which], chunk_rows(chunk)]
+            remote(
+                piece, piece, asend.at[0], arecv.at[which, chunk], (target, dom)
+            ).wait_recv()
+        lax.fori_loop(2 * chunk, 2 * chunk + 2, lambda_rows, 0)
+        natural_order(chunk)
+        each_owner(chunk, lambda copy: copy.start(), True)
+
+    @pl.when(grp != 2)
+    def _():
+        for step in range(2):
+            analyse(turn(step, own_count))
 
     @pl.when(grp < 2)
     def _():
-        for chunk in range(HALF // CHUNK):
-            for which, other in ((0, 1 - grp), (1, 2)):
-                piece = recv.at[other, chunk_rows(chunk)]
-                remote(
-                    piece, piece, asend.at[chunk], arecv.at[which, chunk], (target, dom)
-                ).wait_recv()
-            lax.fori_loop(chunk * CHUNK // 16, (chunk + 1) * CHUNK // 16, lambda_rows, 0)
-            natural_order(chunk)
-            for k in range(chunk * CHUNK // 8, (chunk + 1) * CHUNK // 8):
-                to_owner(k).start()
-        for k in range(HALF // 8):
-            to_owner(k).wait_send()
-
-    for copy in group_copies:
+        analyse(turn(2, own_count))
+
+    @pl.when(grp != 2)
+    def _():
+        for step in range(2):
+            each_owner(turn(step, own_count), lambda copy: copy.wait_send(), False)
+
+    @pl.when(grp < 2)
+    def _():
+        each_owner(turn(2, own_count), lambda copy: copy.wait_send(), False)
+        for copy in second_copies:
+            copy.wait_send()
+
+    for copy in first_copies:
         copy.wait_send()
+
+    def wait_rows(count):
+        piece = lamrecv.at[0 : 8 * count]
+        remote(piece, piece, osend.at[0], orecv, (target, dom)).wait_recv()
+
+    to_itself = lax.rem(lax.div(lax.rem(dom, 8), 2) - lax.div(dom, 8) + 4, 4) == 3
+
+    @pl.when((grp == 3) & to_itself)
+    def _():
+        wait_rows(31)
+
+    @pl.when((grp == 3) & jnp.logical_not(to_itself))
+    def _():
+        wait_rows(32)
 
     @pl.when(grp == 3)
     def _():
-        remote(lamrecv, lamrecv, osend.at[0], orecv, (target, dom)).wait_recv()
         out[...] = lamrecv[...]
 
 
@@ -885,12 +948,12 @@
             pltpu.VMEM((4, 2, LAYER, 128), F32),
             pltpu.VMEM((8, 128), F32),
             pltpu.VMEM((DOMS, 8, 128), F32),
-            pltpu.VMEM((HALF, 3 * NODES), BF16),
-            pltpu.VMEM((3, HALF, 3 * NODES), BF16),
-            pltpu.VMEM((HALF, NODES), F32),
+            pltpu.VMEM((2 * SHARE, 3 * NODES), BF16),
+            pltpu.VMEM((3, SHARE, 3 * NODES), BF16),
+            pltpu.VMEM((SHARE, NODES), F32),
             pltpu.VMEM(own, F32),
             dma((6,)), dma((12,)), dma, dma((2,)), dma((2,)), dma((4,)), dma((4,)), dma((2,)),
-            dma((2,)), dma, dma, dma((HALF // CHUNK,)), dma((2, HALF // CHUNK)), dma((HALF // 8,)), dma,
+            dma((2,)), dma, dma, dma((5,)), dma((2, 3)), dma((12,)), dma,
         ],
         compiler_params=pltpu.CompilerParams(
             collective_id=0, has_side_effects=True, vmem_limit_bytes=60 * 1024 * 1024

time: 50.9 us -> 51.1 us (level)
  the two profiles are of different devices: /device:TPU:15 before, /device:TPU:7 now
where the time goes in v4:
time: 51.1 us; the launch traced here: 51 us
  Pallas kernels  50.2 us (98%)
  local copies, waits for them, and re-layouts  0.8 us (2%)
    pallas_call x1, Pallas kernels, per_device(): pl.pallas_call(kernel, out_shape=pltpu.VMEM(own, F32), in_specs=[hbm] * 8...  50.2 us

profile of v4, /device:TPU:7, one launch (start us, length us, event | category | flops | bytes accessed | tf_op | source)
XLA Modules:
  0.0 51.0 jit_solution(17394728392880930222)
XLA Ops:
  0.0 50.2 %solve_and_analyse.1 = f32[256,512]{1,0:T(8,128)S(1)} custom-call(f32[3,256,512]{2,1,0:T(8,128)} %forcing.1, f32[1,256]{1,0:T(1,128)} %bitcast.4, f32[1,256]{1,0:T(1,128)} %bitcast.5, s32[1,256]{1,0:T(1,128)} %order_in.1, s32[1,256]{1,0:T(1,128)} %owner_in.1, f32[8,512]{1,0:T(8,128)} %constant.6.clone.lanes_in, bf16[640,384]{1,0:T(8,128)(2,1)} %constant.7.clone.flat_in, ...), custom_call_target="tpu_custom_call" | custom-call | tf_op jit(solution)/shard_map/solve_and_analyse/pallas_call | solution.py:913
  50.2 0.8 %copy.10 = f32[1,256,512]{2,1,0:T(8,128)} copy(f32[1,256,512]{2,1,0:T(8,128)S(1)} %bitcast.3) | data formatting | bytes 1048576

commit v5 on v4

--- a/solution.py
+++ b/solution.py
@@ -17,7 +17,7 @@
 NODES = 512
 DOMS = 32
 CHUNK = 32
-SHARE = 96
+SHARE = 64
 BASIS_LOW = 0.3
 BASIS_HIGH = 2.0
 THETA = 0.5 * (BASIS_LOW + BASIS_HIGH)
@@ -675,52 +675,44 @@
                 other = term if other is None else other + term
             mean_face(layer, 0, other, 0.5 * (has_up if side else has_down))
 
-    target = 1 - lax.rem(grp, 2)
-    source = lax.div(grp, 2)
-    own_first = jnp.where(grp == 3, 2, lax.rem(grp, 2)) * SHARE
-    own_count = jnp.where(grp == 3, 2, 3)
-
-    def pack(first, count, into):
-        slots = pl.ds(pl.multiple_of(first, CHUNK), count)
-
-        def body(part, carry):
-            cols = pl.ds(pl.multiple_of(part * 512, 512), 512)
-            into[:, cols] = jnp.dot(
-                gpack[slots, :], gcells[:, cols], preferred_element_type=F32
-            ).astype(BF16)
-            return carry
-
-        lax.fori_loop(0, 3, body, 0)
-
-    def chunk_rows(chunk):
-        return pl.ds(pl.multiple_of(chunk * CHUNK, CHUNK), CHUNK)
-
-    def turn(step, count):
-        return lax.rem(dom + step, count)
-
-    def piece_copy(start, chunk, slot, device, which):
+    own_first = grp * SHARE
+
+    def pack(part, carry):
+        cols = pl.ds(pl.multiple_of(part * 512, 512), 512)
+        packed[:, cols] = jnp.dot(
+            gpack[...], gcells[:, cols], preferred_element_type=F32
+        ).astype(BF16)
+        return carry
+
+    lax.fori_loop(0, 3, pack, 0)
+
+    def chunk_rows(chunk, base=0):
+        return pl.ds(pl.multiple_of(base + chunk * CHUNK, CHUNK), CHUNK)
+
+    def turn(step):
+        return lax.rem(dom + step, 2)
+
+    def piece_copy(step, target, slot):
+        chunk = turn(step)
         return remote(
-            packed.at[chunk_rows(start + chunk)], recv.at[comp, chunk_rows(chunk)],
-            asend.at[slot], arecv.at[which, chunk], (device, dom),
-        )
-
-    pack(target * SHARE, SHARE, packed.at[0:SHARE])
-
-    first_copies = [piece_copy(0, turn(k, 3), k, target, source) for k in range(3)]
-    second_copies = [piece_copy(3, turn(k, 2), 3 + k, 3, grp) for k in range(2)]
-    for copy in first_copies:
-        copy.start()
-
-    @pl.when(grp < 2)
-    def _():
-        pack(2 * SHARE, CELLS - 2 * SHARE, packed.at[SHARE : SHARE + CELLS - 2 * SHARE])
-        for copy in second_copies:
-            copy.start()
-        pack(own_first, SHARE, recv.at[comp])
-
-    @pl.when(grp == 3)
-    def _():
-        pack(own_first, CELLS - 2 * SHARE, recv.at[comp, 0 : CELLS - 2 * SHARE])
+            packed.at[chunk_rows(chunk, target * SHARE)], recv.at[comp, chunk_rows(chunk)],
+            asend.at[slot, step], arecv.at[comp, chunk], (target, dom),
+        )
+
+    def each_send(action):
+        @pl.when(grp < 2)
+        def _():
+            for step in range(2):
+                for hop in (2, 1, 3):
+                    action(piece_copy(step, lax.rem(grp + hop, 4), hop - 1))
+
+        @pl.when(grp >= 2)
+        def _():
+            for step in range(2):
+                action(piece_copy(step, 3 - grp, 0))
+
+    each_send(lambda copy: copy.start())
+    recv[comp] = packed[pl.ds(pl.multiple_of(own_first, SHARE), SHARE), :]
 
     wide8 = [value.reshape(1, 8, 128) for value in coef]
 
@@ -805,42 +797,25 @@
                     lamrecv[here, :] = lam[rows, :]
 
     def analyse(chunk):
-        others = (jnp.where(grp == 0, 1, 0), jnp.where(grp == 3, 1, 2))
-        for which in range(2):
-            piece = recv.at[others[which], chunk_rows(chunk)]
+        for step in (1, 2):
+            other = lax.rem(comp + step, 3)
+            piece = recv.at[other, chunk_rows(chunk)]
             remote(
-                piece, piece, asend.at[0], arecv.at[which, chunk], (target, dom)
+                piece, piece, asend.at[0, 0], arecv.at[other, chunk], (lax.rem(grp + 1, 4), dom)
             ).wait_recv()
         lax.fori_loop(2 * chunk, 2 * chunk + 2, lambda_rows, 0)
         natural_order(chunk)
         each_owner(chunk, lambda copy: copy.start(), True)
 
-    @pl.when(grp != 2)
-    def _():
-        for step in range(2):
-            analyse(turn(step, own_count))
-
-    @pl.when(grp < 2)
-    def _():
-        analyse(turn(2, own_count))
-
-    @pl.when(grp != 2)
-    def _():
-        for step in range(2):
-            each_owner(turn(step, own_count), lambda copy: copy.wait_send(), False)
-
-    @pl.when(grp < 2)
-    def _():
-        each_owner(turn(2, own_count), lambda copy: copy.wait_send(), False)
-        for copy in second_copies:
-            copy.wait_send()
-
-    for copy in first_copies:
-        copy.wait_send()
+    for step in range(2):
+        analyse(turn(step))
+    for step in range(2):
+        each_owner(turn(step), lambda copy: copy.wait_send(), False)
+    each_send(lambda copy: copy.wait_send())
 
     def wait_rows(count):
         piece = lamrecv.at[0 : 8 * count]
-        remote(piece, piece, osend.at[0], orecv, (target, dom)).wait_recv()
+        remote(piece, piece, osend.at[0], orecv, (lax.rem(grp + 1, 4), dom)).wait_recv()
 
     to_itself = lax.rem(lax.div(lax.rem(dom, 8), 2) - lax.div(dom, 8) + 4, 4) == 3
 
@@ -948,12 +923,12 @@
             pltpu.VMEM((4, 2, LAYER, 128), F32),
             pltpu.VMEM((8, 128), F32),
             pltpu.VMEM((DOMS, 8, 128), F32),
-            pltpu.VMEM((2 * SHARE, 3 * NODES), BF16),
+            pltpu.VMEM((CELLS, 3 * NODES), BF16),
             pltpu.VMEM((3, SHARE, 3 * NODES), BF16),
             pltpu.VMEM((SHARE, NODES), F32),
             pltpu.VMEM(own, F32),
             dma((6,)), dma((12,)), dma, dma((2,)), dma((2,)), dma((4,)), dma((4,)), dma((2,)),
-            dma((2,)), dma, dma, dma((5,)), dma((2, 3)), dma((12,)), dma,
+            dma((2,)), dma, dma, dma((3, 2)), dma((3, 2)), dma((8,)), dma,
         ],
         compiler_params=pltpu.CompilerParams(
             collective_id=0, has_side_effects=True, vmem_limit_bytes=60 * 1024 * 1024

time: 51.1 us -> 46.8 us (0.916)
  Pallas kernels: 50.2 us -> 45.8 us
    pallas_call x1, Pallas kernels: 50.2 us -> 45.8 us  [per_device(): pl.pallas_call(kernel, out_shape=pltpu.VMEM(own, F32), in_specs=[hbm] * 8...]
where the time goes in v5:
time: 46.8 us; the launch traced here: 46.6 us
  Pallas kernels  45.8 us (98%)
  local copies, waits for them, and re-layouts  0.8 us (2%)
    pallas_call x1, Pallas kernels, per_device(): pl.pallas_call(kernel, out_shape=pltpu.VMEM(own, F32), in_specs=[hbm] * 8...  45.8 us

profile of v5, /device:TPU:7, one launch (start us, length us, event | category | flops | bytes accessed | tf_op | source)
XLA Modules:
  0.0 46.6 jit_solution(54870610142886668)
XLA Ops:
  0.0 45.8 %solve_and_analyse.1 = f32[256,512]{1,0:T(8,128)S(1)} custom-call(f32[3,256,512]{2,1,0:T(8,128)} %forcing.1, f32[1,256]{1,0:T(1,128)} %bitcast.4, f32[1,256]{1,0:T(1,128)} %bitcast.5, s32[1,256]{1,0:T(1,128)} %order_in.1, s32[1,256]{1,0:T(1,128)} %owner_in.1, f32[8,512]{1,0:T(8,128)} %constant.6.clone.lanes_in, bf16[640,384]{1,0:T(8,128)(2,1)} %constant.7.clone.flat_in, ...), custom_call_target="tpu_custom_call" | custom-call | tf_op jit(solution)/shard_map/solve_and_analyse/pallas_call | solution.py:888
  45.8 0.8 %copy.10 = f32[1,256,512]{2,1,0:T(8,128)} copy(f32[1,256,512]{2,1,0:T(8,128)S(1)} %bitcast.3) | data formatting | bytes 1048576

commit v6 on v5

--- a/solution.py
+++ b/solution.py
@@ -16,7 +16,8 @@
 CELLS = 256
 NODES = 512
 DOMS = 32
-CHUNK = 32
+CHUNK = 16
+PIECES = 4
 SHARE = 64
 BASIS_LOW = 0.3
 BASIS_HIGH = 2.0
@@ -690,7 +691,7 @@
         return pl.ds(pl.multiple_of(base + chunk * CHUNK, CHUNK), CHUNK)
 
     def turn(step):
-        return lax.rem(dom + step, 2)
+        return lax.rem(dom + step, PIECES)
 
     def piece_copy(step, target, slot):
         chunk = turn(step)
@@ -702,13 +703,13 @@
     def each_send(action):
         @pl.when(grp < 2)
         def _():
-            for step in range(2):
+            for step in range(PIECES):
                 for hop in (2, 1, 3):
                     action(piece_copy(step, lax.rem(grp + hop, 4), hop - 1))
 
         @pl.when(grp >= 2)
         def _():
-            for step in range(2):
+            for step in range(PIECES):
                 action(piece_copy(step, 3 - grp, 0))
 
     each_send(lambda copy: copy.start())
@@ -776,16 +777,18 @@
 
     def each_owner(chunk, action, local):
         piece = lax.div(own_first, CHUNK) + chunk
-        for place in range(4):
-            owner = place * 8 + lax.rem(place + lax.div(piece, 2), 4) * 2 + lax.rem(piece, 2)
-            rows = pl.ds(pl.multiple_of(chunk * CHUNK + place * 8, 8), 8)
+        four = lax.div(piece, 2)
+        for part in range(2):
+            place = lax.rem(piece, 2) * 2 + part
+            owner = place * 8 + lax.rem(place + lax.div(four, 2), 4) * 2 + lax.rem(four, 2)
+            rows = pl.ds(pl.multiple_of(chunk * CHUNK + part * 8, 8), 8)
             own = (grp == 3) & (owner == dom)
 
             @pl.when(jnp.logical_not(own))
             def _():
                 action(
                     remote(
-                        lam.at[rows], lamrecv.at[here], osend.at[chunk * 4 + place], orecv,
+                        lam.at[rows], lamrecv.at[here], osend.at[chunk * 2 + part], orecv,
                         (3, owner),
                     )
                 )
@@ -803,13 +806,12 @@
             remote(
                 piece, piece, asend.at[0, 0], arecv.at[other, chunk], (lax.rem(grp + 1, 4), dom)
             ).wait_recv()
-        lax.fori_loop(2 * chunk, 2 * chunk + 2, lambda_rows, 0)
+        lambda_rows(chunk, 0)
         natural_order(chunk)
         each_owner(chunk, lambda copy: copy.start(), True)
 
-    for step in range(2):
-        analyse(turn(step))
-    for step in range(2):
+    over(0, PIECES, lambda step: analyse(turn(step)))
+    for step in range(PIECES):
         each_owner(turn(step), lambda copy: copy.wait_send(), False)
     each_send(lambda copy: copy.wait_send())
 
@@ -928,7 +930,7 @@
             pltpu.VMEM((SHARE, NODES), F32),
             pltpu.VMEM(own, F32),
             dma((6,)), dma((12,)), dma, dma((2,)), dma((2,)), dma((4,)), dma((4,)), dma((2,)),
-            dma((2,)), dma, dma, dma((3, 2)), dma((3, 2)), dma((8,)), dma,
+            dma((2,)), dma, dma, dma((3, PIECES)), dma((3, PIECES)), dma((8,)), dma,
         ],
         compiler_params=pltpu.CompilerParams(
             collective_id=0, has_side_effects=True, vmem_limit_bytes=60 * 1024 * 1024

time: 46.8 us -> 46.3 us (0.989)
  no operation moved by 1% of the time
where the time goes in v6:
time: 46.3 us; the launch traced here: 46.2 us
  Pallas kernels  45.4 us (98%)
  local copies, waits for them, and re-layouts  0.8 us (2%)
    pallas_call x1, Pallas kernels, per_device(): pl.pallas_call(kernel, out_shape=pltpu.VMEM(own, F32), in_specs=[hbm] * 8...  45.4 us

profile of v6, /device:TPU:7, one launch (start us, length us, event | category | flops | bytes accessed | tf_op | source)
XLA Modules:
  0.0 46.2 jit_solution(13938736301782360852)
XLA Ops:
  0.0 45.4 %solve_and_analyse.1 = f32[256,512]{1,0:T(8,128)S(1)} custom-call(f32[3,256,512]{2,1,0:T(8,128)} %forcing.1, f32[1,256]{1,0:T(1,128)} %bitcast.4, f32[1,256]{1,0:T(1,128)} %bitcast.5, s32[1,256]{1,0:T(1,128)} %order_in.1, s32[1,256]{1,0:T(1,128)} %owner_in.1, f32[8,512]{1,0:T(8,128)} %constant.6.clone.lanes_in, bf16[640,384]{1,0:T(8,128)(2,1)} %constant.7.clone.flat_in, ...), custom_call_target="tpu_custom_call" | custom-call | tf_op jit(solution)/shard_map/solve_and_analyse/pallas_call | solution.py:890
  45.4 0.8 %copy.10 = f32[1,256,512]{2,1,0:T(8,128)} copy(f32[1,256,512]{2,1,0:T(8,128)S(1)} %bitcast.3) | data formatting | bytes 1048576

commit v7 on v6

--- a/solution.py
+++ b/solution.py
@@ -119,7 +119,7 @@
     forcing, visc_in, mass_in, order_in, owner_in, lanes_in, flat_in, mats,
     out,
     fsc, lanes, flat, order_sc, owner_sc, weights, par, parn, pone, ptr, parts, visc, mass, raw, tmp,
-    inv, lhs, v0, v1, v2, v3, xs, xstd, grads, gpack, classes, gcells, fsend, frecv, fghost, moments,
+    inv, lhs0, lhs1, lhs2, lhs3, v0, v1, v2, v3, xs, xstd, grads, gpack, classes, gcells, fsend, frecv, fghost, moments,
     red, packed, recv, lam, lamrecv,
     ssem, wsem, fsem, psend, precv, gsend, grecv, f3send, f3recv, rsend, rrecv, asend, arecv,
     osend, orecv,
@@ -131,6 +131,7 @@
     down = lax.rem(dom + DOMS - 1, DOMS)
     barrier = pltpu.get_barrier_semaphore()
     basis = (v0, v1, v2, v3)
+    lefts = (lhs0, lhs1, lhs2, lhs3)
     every = (0, 1, 2, 3)
 
     for step in range(1, DOMS):
@@ -230,7 +231,7 @@
         high = value.astype(BF16)
         return high, (value - high.astype(F32)).astype(BF16)
 
-    def store_lhs(layer, pair, first, second):
+    def store_lhs(lhs, layer, pair, first, second):
         for start, value in ((0, first + second), (768, first - second)):
             start = start + pair * 128
             high, low = split(value.reshape(LAYER, 128))
@@ -301,25 +302,28 @@
         remote(par, parn.at[0], psend.at[0], precv.at[0], (grp, up)),
         remote(par, parn.at[1], psend.at[1], precv.at[1], (grp, down)),
     ]
-    ghost_copies = [
-        remote(
-            raw.at[5 * LAYER : 8 * LAYER], raw.at[1 * LAYER : 4 * LAYER],
-            gsend.at[0], grecv.at[0], (grp, up),
-        ),
-        remote(
-            raw.at[4 * LAYER : 7 * LAYER], raw.at[8 * LAYER : 11 * LAYER],
-            gsend.at[1], grecv.at[1], (grp, down),
-        ),
-        remote(
-            raw.at[4 * LAYER : 5 * LAYER, 384:512], raw.at[0:LAYER, 384:512],
-            gsend.at[2], grecv.at[2], (grp, up),
-        ),
-        remote(
-            raw.at[7 * LAYER : 8 * LAYER, 384:512], raw.at[11 * LAYER : 12 * LAYER, 384:512],
-            gsend.at[3], grecv.at[3], (grp, down),
-        ),
+    def ghost(source, layers, first, last, target, slot, device):
+        return remote(
+            raw.at[source * LAYER : (source + layers) * LAYER, first:last],
+            raw.at[target * LAYER : (target + layers) * LAYER, first:last],
+            gsend.at[slot], grecv.at[slot], (grp, device),
+        )
+
+    near_copies = [
+        ghost(7, 1, 0, 512, 3, 0, up),
+        ghost(4, 1, 0, 512, 8, 1, down),
+        ghost(6, 1, 384, 512, 2, 2, up),
+        ghost(5, 1, 384, 512, 9, 3, down),
     ]
-    for copy in par_copies + ghost_copies:
+    far_copies = [
+        ghost(6, 1, 0, 384, 2, 4, up),
+        ghost(5, 1, 0, 384, 9, 5, down),
+        ghost(5, 1, 0, 512, 1, 6, up),
+        ghost(6, 1, 0, 512, 10, 7, down),
+        ghost(4, 1, 384, 512, 0, 8, up),
+        ghost(7, 1, 384, 512, 11, 9, down),
+    ]
+    for copy in par_copies + near_copies + far_copies:
         copy.start()
 
     coefficients(par, CELLS, 1.0)
@@ -386,13 +390,16 @@
 
     over(1, 11, diagonal_faces)
 
+    def first_value(layer, tile, force):
+        value = force * load(inv, layer, tile) * (0.5 * DELTA)
+        store(v0, layer, tile, value)
+        return value
+
     def put_first(layer, pair, forces):
-        values = []
-        for tile, force in zip((pair, 3 - pair), forces):
-            value = force * load(inv, layer, tile) * (0.5 * DELTA)
-            store(v0, layer, tile, value)
-            values.append(value)
-        store_lhs(layer, pair, *values)
+        values = [
+            first_value(layer, tile, force) for tile, force in zip((pair, 3 - pair), forces)
+        ]
+        store_lhs(lhs0, layer, pair, *values)
 
     def assemble(layer, tiles, scale):
         sums = []
@@ -411,19 +418,7 @@
     over(4, 8, lambda layer: assemble(layer, every, None))
     for copy in load_mats:
         copy.wait()
-    for copy in ghost_copies:
-        copy.wait()
-    assemble(0, (3,), has_down)
-    over(1, 4, lambda layer: assemble(layer, every, has_down))
-    over(8, 11, lambda layer: assemble(layer, every, has_up))
-    assemble(11, (3,), has_up)
-
-    def first_faces(layer):
-        put_first(layer, 0, [face_sum(tmp, layer, tile) for tile in (0, 3)])
-
-    over(1, 11, first_faces)
-
-    def multiply(low, high, which, target, first=0):
+    def multiply(lhs, low, high, which, target, first=0):
         for part in range(2):
             target[:, first + part * 256 : first + part * 256 + 256] = jnp.dot(
                 lhs[low * LAYER : high * LAYER, part * 768 : part * 768 + 768],
@@ -443,7 +438,7 @@
                 value = value - load(basis[step - 1], layer, tile)
             store(basis[step + 1], layer, tile, value)
             values.append(value)
-        store_lhs(layer, pair, *values)
+        store_lhs(lefts[step + 1], layer, pair, *values)
 
     def apply(step, layer, tiles, sums, going):
         coef_v = column(visc, layer)
@@ -480,23 +475,74 @@
         advance(step, layer, 0, [face_sum(tmp, layer, tile) for tile in (0, 3)])
 
     blank_sums = (jnp.zeros((8, 128), F32), jnp.zeros((8, 128), F32))
-    for step in range(ITERS):
+
+    def own_apply(step, going):
+        sums = lax.fori_loop(
+            4, 8, lambda layer, carry: apply(step, layer, every, carry, going), blank_sums
+        )
+        moments[step : step + 1, :] = jnp.sum(sums[0], axis=0, keepdims=True)
+        moments[4 + step : 5 + step, :] = jnp.sum(sums[1], axis=0, keepdims=True)
+
+    def first_faces(layer):
+        put_first(layer, 0, [face_sum(tmp, layer, tile) for tile in (0, 3)])
+
+    for copy in near_copies:
+        copy.wait()
+    assemble(2, (3,), has_down)
+    assemble(3, every, has_down)
+    assemble(8, every, has_up)
+    assemble(9, (3,), has_up)
+    over(3, 9, first_faces)
+    for layer in (2, 9):
+        first_value(layer, 3, face_sum(tmp, layer, 3))
+    multiply(lhs0, 3, 9, 0, tmp.at[3 * LAYER : 9 * LAYER])
+    own_apply(0, True)
+    for layer in (3, 8):
+        apply(0, layer, every, None, True)
+
+    for copy in far_copies:
+        copy.wait()
+    assemble(0, (3,), has_down)
+    assemble(1, every, has_down)
+    assemble(2, (0, 1, 2), has_down)
+    assemble(9, (0, 1, 2), has_up)
+    assemble(10, every, has_up)
+    assemble(11, (3,), has_up)
+    for layer in (1, 10):
+        first_faces(layer)
+    for layer in (2, 9):
+        value = first_value(layer, 0, face_sum(tmp, layer, 0))
+        store_lhs(lhs0, layer, 0, value, load(v0, layer, 3))
+    far_rows = (slice(1 * LAYER, 3 * LAYER), slice(9 * LAYER, 11 * LAYER))
+    for part in range(2):
+        product = jnp.dot(
+            jnp.concatenate(
+                [lhs0[rows, part * 768 : part * 768 + 768] for rows in far_rows], 0
+            ),
+            weights[part],
+            preferred_element_type=F32,
+        )
+        for side, rows in enumerate(far_rows):
+            tmp[rows, part * 256 : part * 256 + 256] = product[
+                side * 2 * LAYER : (side + 1) * 2 * LAYER
+            ]
+    apply(0, 1, (0,), None, True)
+    apply(0, 2, every, None, True)
+    apply(0, 9, every, None, True)
+    apply(0, 10, (0,), None, True)
+    over(2, 10, lambda layer: faces(0, layer))
+
+    for step in range(1, ITERS):
         low, high = 1 + step, 11 - step
         going = step + 1 < ITERS
-        multiply(low, high, 0, tmp.at[low * LAYER : high * LAYER])
+        multiply(lefts[step], low, high, 0, tmp.at[low * LAYER : high * LAYER])
+        own_apply(step, going)
         if going:
             inward = 0 if low % 2 else 3
             apply(step, low, (inward,), None, True)
             over(low + 1, 4, lambda layer: apply(step, layer, every, None, True))
-        sums = lax.fori_loop(
-            4, 8, lambda layer, carry: apply(step, layer, every, carry, going), blank_sums
-        )
-        if going:
             over(8, high - 1, lambda layer: apply(step, layer, every, None, True))
             apply(step, high - 1, (inward,), None, True)
-        moments[step : step + 1, :] = jnp.sum(sums[0], axis=0, keepdims=True)
-        moments[4 + step : 5 + step, :] = jnp.sum(sums[1], axis=0, keepdims=True)
-        if going:
             over(low + 1, high - 1, lambda layer: faces(step, layer))
 
     red[0] = moments[...]
@@ -522,27 +568,12 @@
         copy.start()
 
     own_rows = slice(4 * LAYER, 8 * LAYER)
-    for index in (3, 0, 1, 2):
-        if index < 3:
-            over(
-                4,
-                8,
-                lambda layer: [
-                    store_lhs(
-                        layer,
-                        pair,
-                        load(basis[index], layer, pair),
-                        load(basis[index], layer, 3 - pair),
-                    )
-                    for pair in (0, 1)
-                ],
-            )
-
+    for index in range(ITERS):
         left = jnp.concatenate(
             [
                 jnp.concatenate(
                     [
-                        lhs[own_rows, start + part * 256 : start + part * 256 + 128]
+                        lefts[index][own_rows, start + part * 256 : start + part * 256 + 128]
                         for part in range(3)
                     ],
                     1,
@@ -556,7 +587,7 @@
             rows = slice(part * CELLS, part * CELLS + CELLS)
             grads[index, :, part * 128 : part * 128 + 128] = both[rows, 0:128]
             grads[index, :, NODES + part * 128 : NODES + part * 128 + 128] = both[rows, 128:256]
-        multiply(4, 8, 1, grads.at[index], 2 * NODES)
+        multiply(lefts[index], 4, 8, 1, grads.at[index], 2 * NODES)
         if index < 3:
             fghost[index, 0] = end_face(basis[index], 3).reshape(LAYER, 128)
             fghost[index, 1] = end_face(basis[index], 8).reshape(LAYER, 128)
@@ -910,6 +941,9 @@
             pltpu.VMEM(wide, F32),
             pltpu.VMEM(wide, F32),
             pltpu.VMEM((12 * LAYER, 3 * NODES), BF16),
+            pltpu.VMEM((12 * LAYER, 3 * NODES), BF16),
+            pltpu.VMEM((12 * LAYER, 3 * NODES), BF16),
+            pltpu.VMEM((12 * LAYER, 3 * NODES), BF16),
             pltpu.VMEM(wide, F32),
             pltpu.VMEM(wide, F32),
             pltpu.VMEM(wide, F32),
@@ -929,7 +963,7 @@
             pltpu.VMEM((3, SHARE, 3 * NODES), BF16),
             pltpu.VMEM((SHARE, NODES), F32),
             pltpu.VMEM(own, F32),
-            dma((6,)), dma((12,)), dma, dma((2,)), dma((2,)), dma((4,)), dma((4,)), dma((2,)),
+            dma((6,)), dma((12,)), dma, dma((2,)), dma((2,)), dma((10,)), dma((10,)), dma((2,)),
             dma((2,)), dma, dma, dma((3, PIECES)), dma((3, PIECES)), dma((8,)), dma,
         ],
         compiler_params=pltpu.CompilerParams(

time: 46.3 us -> 45 us (0.972)
  Pallas kernels: 45.4 us -> 44.1 us
    pallas_call x1, Pallas kernels: 45.4 us -> 44.1 us  [per_device(): pl.pallas_call(kernel, out_shape=pltpu.VMEM(own, F32), in_specs=[hbm] * 8...]
where the time goes in v7:
time: 45 us; the launch traced here: 44.9 us
  Pallas kernels  44.1 us (98%)
  local copies, waits for them, and re-layouts  0.8 us (2%)
    pallas_call x1, Pallas kernels, per_device(): pl.pallas_call(kernel, out_shape=pltpu.VMEM(own, F32), in_specs=[hbm] * 8...  44.1 us

profile of v7, /device:TPU:7, one launch (start us, length us, event | category | flops | bytes accessed | tf_op | source)
XLA Modules:
  0.0 44.9 jit_solution(16170491219704807211)
XLA Ops:
  0.0 44.1 %solve_and_analyse.1 = f32[256,512]{1,0:T(8,128)S(1)} custom-call(f32[3,256,512]{2,1,0:T(8,128)} %forcing.1, f32[1,256]{1,0:T(1,128)} %bitcast.4, f32[1,256]{1,0:T(1,128)} %bitcast.5, s32[1,256]{1,0:T(1,128)} %order_in.1, s32[1,256]{1,0:T(1,128)} %owner_in.1, f32[8,512]{1,0:T(8,128)} %constant.6.clone.lanes_in, bf16[640,384]{1,0:T(8,128)(2,1)} %constant.7.clone.flat_in, ...), custom_call_target="tpu_custom_call" | custom-call | tf_op jit(solution)/shard_map/solve_and_analyse/pallas_call | solution.py:921
  44.1 0.8 %copy.10 = f32[1,256,512]{2,1,0:T(8,128)} copy(f32[1,256,512]{2,1,0:T(8,128)S(1)} %bitcast.3) | data formatting | bytes 1048576

commit v8 on v7

--- a/solution.py
+++ b/solution.py
@@ -17,8 +17,9 @@
 NODES = 512
 DOMS = 32
 CHUNK = 16
-PIECES = 4
-SHARE = 64
+COUNTS = (4, 5, 4, 3)
+FIRSTS = (0, 4, 9, 13)
+MOST = max(COUNTS)
 BASIS_LOW = 0.3
 BASIS_HIGH = 2.0
 THETA = 0.5 * (BASIS_LOW + BASIS_HIGH)
@@ -707,7 +708,14 @@
                 other = term if other is None else other + term
             mean_face(layer, 0, other, 0.5 * (has_up if side else has_down))
 
-    own_first = grp * SHARE
+    def by_row(values):
+        picked = values[3]
+        for row in (2, 1, 0):
+            picked = jnp.where(grp == row, values[row], picked)
+        return picked
+
+    own_first = by_row([first * CHUNK for first in FIRSTS])
+    own_count = by_row(COUNTS)
 
     def pack(part, carry):
         cols = pl.ds(pl.multiple_of(part * 512, 512), 512)
@@ -721,30 +729,35 @@
     def chunk_rows(chunk, base=0):
         return pl.ds(pl.multiple_of(base + chunk * CHUNK, CHUNK), CHUNK)
 
-    def turn(step):
-        return lax.rem(dom + step, PIECES)
+    def turn(step, count):
+        return lax.rem(dom + step, count)
 
     def piece_copy(step, target, slot):
-        chunk = turn(step)
+        chunk = turn(step, COUNTS[target])
         return remote(
-            packed.at[chunk_rows(chunk, target * SHARE)], recv.at[comp, chunk_rows(chunk)],
+            packed.at[chunk_rows(chunk, FIRSTS[target] * CHUNK)],
+            recv.at[comp, chunk_rows(chunk)],
             asend.at[slot, step], arecv.at[comp, chunk], (target, dom),
         )
 
     def each_send(action):
-        @pl.when(grp < 2)
+        for row, targets in enumerate(((2, 1, 3), (3, 2, 0), (1,), (0,))):
+
+            @pl.when(grp == row)
+            def _():
+                for step in range(MOST):
+                    for slot, target in enumerate(targets):
+                        if step < COUNTS[target]:
+                            action(piece_copy(step, target, slot))
+
+    each_send(lambda copy: copy.start())
+    for row in range(4):
+
+        @pl.when(grp == row)
         def _():
-            for step in range(PIECES):
-                for hop in (2, 1, 3):
-                    action(piece_copy(step, lax.rem(grp + hop, 4), hop - 1))
-
-        @pl.when(grp >= 2)
-        def _():
-            for step in range(PIECES):
-                action(piece_copy(step, 3 - grp, 0))
-
-    each_send(lambda copy: copy.start())
-    recv[comp] = packed[pl.ds(pl.multiple_of(own_first, SHARE), SHARE), :]
+            slots = COUNTS[row] * CHUNK
+            first = FIRSTS[row] * CHUNK
+            recv[min(row, 2), 0:slots] = packed[first : first + slots, :]
 
     wide8 = [value.reshape(1, 8, 128) for value in coef]
 
@@ -841,16 +854,20 @@
         natural_order(chunk)
         each_owner(chunk, lambda copy: copy.start(), True)
 
-    over(0, PIECES, lambda step: analyse(turn(step)))
-    for step in range(PIECES):
-        each_owner(turn(step), lambda copy: copy.wait_send(), False)
+    over(0, own_count, lambda step: analyse(turn(step, own_count)))
+    over(
+        0,
+        own_count,
+        lambda step: each_owner(turn(step, own_count), lambda copy: copy.wait_send(), False),
+    )
     each_send(lambda copy: copy.wait_send())
 
     def wait_rows(count):
         piece = lamrecv.at[0 : 8 * count]
         remote(piece, piece, osend.at[0], orecv, (lax.rem(grp + 1, 4), dom)).wait_recv()
 
-    to_itself = lax.rem(lax.div(lax.rem(dom, 8), 2) - lax.div(dom, 8) + 4, 4) == 3
+    four = lax.rem(lax.div(lax.rem(dom, 8), 2) - lax.div(dom, 8) + 4, 4) * 2 + lax.rem(dom, 2)
+    to_itself = four * 2 + lax.div(dom, 16) >= FIRSTS[3]
 
     @pl.when((grp == 3) & to_itself)
     def _():
@@ -960,11 +977,11 @@
             pltpu.VMEM((8, 128), F32),
             pltpu.VMEM((DOMS, 8, 128), F32),
             pltpu.VMEM((CELLS, 3 * NODES), BF16),
-            pltpu.VMEM((3, SHARE, 3 * NODES), BF16),
-            pltpu.VMEM((SHARE, NODES), F32),
+            pltpu.VMEM((3, MOST * CHUNK, 3 * NODES), BF16),
+            pltpu.VMEM((MOST * CHUNK, NODES), F32),
             pltpu.VMEM(own, F32),
             dma((6,)), dma((12,)), dma, dma((2,)), dma((2,)), dma((10,)), dma((10,)), dma((2,)),
-            dma((2,)), dma, dma, dma((3, PIECES)), dma((3, PIECES)), dma((8,)), dma,
+            dma((2,)), dma, dma, dma((3, MOST)), dma((3, MOST)), dma((2 * MOST,)), dma,
         ],
         compiler_params=pltpu.CompilerParams(
             collective_id=0, has_side_effects=True, vmem_limit_bytes=60 * 1024 * 1024

time: 45 us -> 43.4 us (0.964)
  Pallas kernels: 44.1 us -> 42.3 us
    pallas_call x1, Pallas kernels: 44.1 us -> 42.3 us  [per_device(): pl.pallas_call(kernel, out_shape=pltpu.VMEM(own, F32), in_specs=[hbm] * 8...]
where the time goes in v8:
time: 43.4 us; the launch traced here: 43.1 us
  Pallas kernels  42.3 us (97%)
  local copies, waits for them, and re-layouts  0.8 us (2%)
    pallas_call x1, Pallas kernels, per_device(): pl.pallas_call(kernel, out_shape=pltpu.VMEM(own, F32), in_specs=[hbm] * 8...  42.3 us

profile of v8, /device:TPU:7, one launch (start us, length us, event | category | flops | bytes accessed | tf_op | source)
XLA Modules:
  0.0 43.1 jit_solution(2451240140175561505)
XLA Ops:
  0.0 42.3 %solve_and_analyse.1 = f32[256,512]{1,0:T(8,128)S(1)} custom-call(f32[3,256,512]{2,1,0:T(8,128)} %forcing.1, f32[1,256]{1,0:T(1,128)} %bitcast.4, f32[1,256]{1,0:T(1,128)} %bitcast.5, s32[1,256]{1,0:T(1,128)} %order_in.1, s32[1,256]{1,0:T(1,128)} %owner_in.1, f32[8,512]{1,0:T(8,128)} %constant.6.clone.lanes_in, bf16[640,384]{1,0:T(8,128)(2,1)} %constant.7.clone.flat_in, ...), custom_call_target="tpu_custom_call" | custom-call | tf_op jit(solution)/shard_map/solve_and_analyse/pallas_call | solution.py:938
  42.3 0.8 %copy.10 = f32[1,256,512]{2,1,0:T(8,128)} copy(f32[1,256,512]{2,1,0:T(8,128)S(1)} %bitcast.3) | data formatting | bytes 1048576

commit v9 on v8

--- a/solution.py
+++ b/solution.py
@@ -135,10 +135,20 @@
     lefts = (lhs0, lhs1, lhs2, lhs3)
     every = (0, 1, 2, 3)
 
-    for step in range(1, DOMS):
-        pl.semaphore_signal(
-            barrier, inc=1, device_id=(grp, lax.rem(dom + step, DOMS)), device_id_type=MESH
-        )
+    at_y = [lax.rem(lax.div(dom, 8) + k, 4) * 8 for k in range(4)]
+    at_z = [lax.rem(lax.div(dom, 2) + k, 4) * 2 for k in range(4)]
+    at_core = [lax.rem(dom + k, 2) for k in range(2)]
+
+    def hops(offset):
+        return sum(min(k, 4 - k) for k in (offset // 8, offset // 2 % 4))
+
+    peers = [
+        (offset, at_y[offset // 8] + at_z[offset // 2 % 4] + at_core[offset % 2])
+        for offset in sorted(range(1, DOMS), key=lambda offset: -hops(offset))
+    ]
+
+    for offset, peer in peers:
+        pl.semaphore_signal(barrier, inc=1, device_id=(grp, peer), device_id_type=MESH)
     for step in range(1, 4):
         pl.semaphore_signal(
             barrier, inc=1, device_id=(lax.rem(grp + step, 4), dom), device_id_type=MESH
@@ -547,10 +557,8 @@
             over(low + 1, high - 1, lambda layer: faces(step, layer))
 
     red[0] = moments[...]
-    for step in range(1, DOMS):
-        remote(
-            moments, red.at[step], rsend, rrecv, (grp, lax.rem(dom + step, DOMS))
-        ).start()
+    for offset, peer in peers:
+        remote(moments, red.at[offset], rsend, rrecv, (grp, peer)).start()
 
     def end_face(ref, layer):
         total = load(ref, layer, 0) * table(2, 0)

time: 43.4 us -> 43.5 us (level); the launches traced: 43.1 us -> 42.7 us
  no operation moved by 1% of the time
where the time goes in v9:
time: 43.5 us; the launch traced here: 42.7 us
  Pallas kernels  41.9 us (96%)
  local copies, waits for them, and re-layouts  0.8 us (2%)
    pallas_call x1, Pallas kernels, per_device(): pl.pallas_call(kernel, out_shape=pltpu.VMEM(own, F32), in_specs=[hbm] * 8...  41.9 us

profile of v9, /device:TPU:7, one launch (start us, length us, event | category | flops | bytes accessed | tf_op | source)
XLA Modules:
  0.0 42.7 jit_solution(2168243544684498139)
XLA Ops:
  0.0 41.9 %solve_and_analyse.1 = f32[256,512]{1,0:T(8,128)S(1)} custom-call(f32[3,256,512]{2,1,0:T(8,128)} %forcing.1, f32[1,256]{1,0:T(1,128)} %bitcast.4, f32[1,256]{1,0:T(1,128)} %bitcast.5, s32[1,256]{1,0:T(1,128)} %order_in.1, s32[1,256]{1,0:T(1,128)} %owner_in.1, f32[8,512]{1,0:T(8,128)} %constant.6.clone.lanes_in, bf16[640,384]{1,0:T(8,128)(2,1)} %constant.7.clone.flat_in, ...), custom_call_target="tpu_custom_call" | custom-call | tf_op jit(solution)/shard_map/solve_and_analyse/pallas_call | solution.py:946
  41.9 0.8 %copy.10 = f32[1,256,512]{2,1,0:T(8,128)} copy(f32[1,256,512]{2,1,0:T(8,128)S(1)} %bitcast.3) | data formatting | bytes 1048576

commit v10 on v9

--- a/solution.py
+++ b/solution.py
@@ -17,8 +17,8 @@
 NODES = 512
 DOMS = 32
 CHUNK = 16
-COUNTS = (4, 5, 4, 3)
-FIRSTS = (0, 4, 9, 13)
+COUNTS = (5, 5, 4, 2)
+FIRSTS = (0, 5, 10, 14)
 MOST = max(COUNTS)
 BASIS_LOW = 0.3
 BASIS_HIGH = 2.0
@@ -788,15 +788,11 @@
 
     def lambda_rows(block, carry):
         rows = pl.ds(pl.multiple_of(block * 16, 16), 16)
-        for part in range(2):
-            jac = [
-                [
-                    recv[c, rows, d * NODES + part * 256 : d * NODES + part * 256 + 256].astype(F32)
-                    for d in range(3)
-                ]
-                for c in range(3)
-            ]
-            lam[rows, part * 256 : part * 256 + 256] = lambda_two(jac)
+        jac = [
+            [recv[c, rows, d * NODES : d * NODES + NODES].astype(F32) for d in range(3)]
+            for c in range(3)
+        ]
+        lam[rows, :] = lambda_two(jac)
         return carry
 
     def natural_order(chunk):

time: 43.5 us -> 43.7 us (level)
  Pallas kernels: 41.9 us -> 42.5 us
    pallas_call x1, Pallas kernels: 41.9 us -> 42.5 us  [per_device(): pl.pallas_call(kernel, out_shape=pltpu.VMEM(own, F32), in_specs=[hbm] * 8...]
where the time goes in v10:
time: 43.7 us; the launch traced here: 43.3 us
  Pallas kernels  42.5 us (97%)
  local copies, waits for them, and re-layouts  0.8 us (2%)
    pallas_call x1, Pallas kernels, per_device(): pl.pallas_call(kernel, out_shape=pltpu.VMEM(own, F32), in_specs=[hbm] * 8...  42.5 us

profile of v10, /device:TPU:7, one launch (start us, length us, event | category | flops | bytes accessed | tf_op | source)
XLA Modules:
  0.0 43.3 jit_solution(13364505928678453038)
XLA Ops:
  0.0 42.5 %solve_and_analyse.1 = f32[256,512]{1,0:T(8,128)S(1)} custom-call(f32[3,256,512]{2,1,0:T(8,128)} %forcing.1, f32[1,256]{1,0:T(1,128)} %bitcast.4, f32[1,256]{1,0:T(1,128)} %bitcast.5, s32[1,256]{1,0:T(1,128)} %order_in.1, s32[1,256]{1,0:T(1,128)} %owner_in.1, f32[8,512]{1,0:T(8,128)} %constant.6.clone.lanes_in, bf16[640,384]{1,0:T(8,128)(2,1)} %constant.7.clone.flat_in, ...), custom_call_target="tpu_custom_call" | custom-call | tf_op jit(solution)/shard_map/solve_and_analyse/pallas_call | solution.py:942
  42.5 0.8 %copy.10 = f32[1,256,512]{2,1,0:T(8,128)} copy(f32[1,256,512]{2,1,0:T(8,128)S(1)} %bitcast.3) | data formatting | bytes 1048576

commit v11 on v10

--- a/solution.py
+++ b/solution.py
@@ -274,7 +274,11 @@
             store(target, base + layer, place, mixed)
 
     def over(low, high, body):
-        lax.fori_loop(low, high, lambda layer, carry: (body(layer), carry)[1], 0)
+        if isinstance(high, int):
+            for layer in range(low, high):
+                body(layer)
+        else:
+            lax.fori_loop(low, high, lambda layer, carry: (body(layer), carry)[1], 0)
 
     cell_sub = lax.broadcasted_iota(jnp.int32, (CELLS, CELLS), 0).astype(F32)
     cell_lane = lax.broadcasted_iota(jnp.int32, (CELLS, CELLS), 1).astype(F32)
@@ -488,9 +492,9 @@
     blank_sums = (jnp.zeros((8, 128), F32), jnp.zeros((8, 128), F32))
 
     def own_apply(step, going):
-        sums = lax.fori_loop(
-            4, 8, lambda layer, carry: apply(step, layer, every, carry, going), blank_sums
-        )
+        sums = blank_sums
+        for layer in range(4, 8):
+            sums = apply(step, layer, every, sums, going)
         moments[step : step + 1, :] = jnp.sum(sums[0], axis=0, keepdims=True)
         moments[4 + step : 5 + step, :] = jnp.sum(sums[1], axis=0, keepdims=True)
 
@@ -687,7 +691,7 @@
         gcells[rows_of(layer), start : start + 128] = value.reshape(LAYER, 128).astype(BF16)
 
     def flat_grads(layer):
-        z_sign = (1 - 2 * lax.rem(layer, 2)).astype(F32)
+        z_sign = -1.0 if layer % 2 else 1.0
         for pair in (0, 1):
             for tile, value in zip((pair, 3 - pair), combined(layer, 0, pair)):
                 put_grad(layer, 0, tile, x_scale * (value - x_others(value)))

time: 43.7 us -> 43.3 us (level)
  no operation moved by 1% of the time
where the time goes in v11:
time: 43.3 us; the launch traced here: 43.1 us
  Pallas kernels  42.3 us (98%)
  local copies, waits for them, and re-layouts  0.8 us (2%)
    pallas_call x1, Pallas kernels, per_device(): pl.pallas_call(kernel, out_shape=pltpu.VMEM(own, F32), in_specs=[hbm] * 8...  42.3 us

profile of v11, /device:TPU:7, one launch (start us, length us, event | category | flops | bytes accessed | tf_op | source)
XLA Modules:
  0.0 43.1 jit_solution(13219818006513570126)
XLA Ops:
  0.0 42.3 %solve_and_analyse.1 = f32[256,512]{1,0:T(8,128)S(1)} custom-call(f32[3,256,512]{2,1,0:T(8,128)} %forcing.1, f32[1,256]{1,0:T(1,128)} %bitcast.4, f32[1,256]{1,0:T(1,128)} %bitcast.5, s32[1,256]{1,0:T(1,128)} %order_in.1, s32[1,256]{1,0:T(1,128)} %owner_in.1, f32[8,512]{1,0:T(8,128)} %constant.6.clone.lanes_in, bf16[640,384]{1,0:T(8,128)(2,1)} %constant.7.clone.flat_in, ...), custom_call_target="tpu_custom_call" | custom-call | tf_op jit(solution)/shard_map/solve_and_analyse/pallas_call | solution.py:946
  42.3 0.8 %copy.10 = f32[1,256,512]{2,1,0:T(8,128)} copy(f32[1,256,512]{2,1,0:T(8,128)S(1)} %bitcast.3) | data formatting | bytes 1048576

commit v12 on v11

--- a/solution.py
+++ b/solution.py
@@ -690,19 +690,25 @@
         start = direction * NODES + tile * 128
         gcells[rows_of(layer), start : start + 128] = value.reshape(LAYER, 128).astype(BF16)
 
-    def flat_grads(layer):
+    def pack(direction):
+        cols = slice(direction * NODES, direction * NODES + NODES)
+        packed[:, cols] = jnp.dot(
+            gpack[...], gcells[:, cols], preferred_element_type=F32
+        ).astype(BF16)
+
+    for direction, scale, others in ((0, x_scale, x_others), (1, y_scale, y_others)):
+        for layer in range(4):
+            for pair in (0, 1):
+                for tile, value in zip((pair, 3 - pair), combined(layer, direction, pair)):
+                    put_grad(layer, direction, tile, scale * (value - others(value)))
+        pack(direction)
+
+    for layer in range(4):
         z_sign = -1.0 if layer % 2 else 1.0
-        for pair in (0, 1):
-            for tile, value in zip((pair, 3 - pair), combined(layer, 0, pair)):
-                put_grad(layer, 0, tile, x_scale * (value - x_others(value)))
-            for tile, value in zip((pair, 3 - pair), combined(layer, 1, pair)):
-                put_grad(layer, 1, tile, y_scale * (value - y_others(value)))
         for tile, value in zip((1, 2), combined(layer, 2, 1)):
             put_grad(layer, 2, tile, z_sign * value)
         for tile, value in zip((0, 3), combined(layer, 2, 0)):
             store(xstd, layer, tile, z_sign * value)
-
-    over(0, 4, flat_grads)
 
     def mean_face(layer, tile, other, there):
         value = load(xstd, layer, tile)
@@ -729,14 +735,7 @@
     own_first = by_row([first * CHUNK for first in FIRSTS])
     own_count = by_row(COUNTS)
 
-    def pack(part, carry):
-        cols = pl.ds(pl.multiple_of(part * 512, 512), 512)
-        packed[:, cols] = jnp.dot(
-            gpack[...], gcells[:, cols], preferred_element_type=F32
-        ).astype(BF16)
-        return carry
-
-    lax.fori_loop(0, 3, pack, 0)
+    pack(2)
 
     def chunk_rows(chunk, base=0):
         return pl.ds(pl.multiple_of(base + chunk * CHUNK, CHUNK), CHUNK)

time: 43.3 us -> 42.7 us (0.986)
  Pallas kernels: 42.3 us -> 41.4 us
    pallas_call x1, Pallas kernels: 42.3 us -> 41.4 us  [per_device(): pl.pallas_call(kernel, out_shape=pltpu.VMEM(own, F32), in_specs=[hbm] * 8...]
where the time goes in v12:
time: 42.7 us; the launch traced here: 42.2 us
  Pallas kernels  41.4 us (97%)
  local copies, waits for them, and re-layouts  0.8 us (2%)
    pallas_call x1, Pallas kernels, per_device(): pl.pallas_call(kernel, out_shape=pltpu.VMEM(own, F32), in_specs=[hbm] * 8...  41.4 us

profile of v12, /device:TPU:7, one launch (start us, length us, event | category | flops | bytes accessed | tf_op | source)
XLA Modules:
  0.0 42.2 jit_solution(3928828202330250791)
XLA Ops:
  0.0 41.4 %solve_and_analyse.1 = f32[256,512]{1,0:T(8,128)S(1)} custom-call(f32[3,256,512]{2,1,0:T(8,128)} %forcing.1, f32[1,256]{1,0:T(1,128)} %bitcast.4, f32[1,256]{1,0:T(1,128)} %bitcast.5, s32[1,256]{1,0:T(1,128)} %order_in.1, s32[1,256]{1,0:T(1,128)} %owner_in.1, f32[8,512]{1,0:T(8,128)} %constant.6.clone.lanes_in, bf16[640,384]{1,0:T(8,128)(2,1)} %constant.7.clone.flat_in, ...), custom_call_target="tpu_custom_call" | custom-call | tf_op jit(solution)/shard_map/solve_and_analyse/pallas_call | solution.py:945
  41.4 0.8 %copy.10 = f32[1,256,512]{2,1,0:T(8,128)} copy(f32[1,256,512]{2,1,0:T(8,128)S(1)} %bitcast.3) | data formatting | bytes 1048576

commit v13 on v12

--- a/solution.py
+++ b/solution.py
@@ -550,7 +550,8 @@
     for step in range(1, ITERS):
         low, high = 1 + step, 11 - step
         going = step + 1 < ITERS
-        multiply(lefts[step], low, high, 0, tmp.at[low * LAYER : high * LAYER])
+        multiply(lefts[step], low, 6, 0, tmp.at[low * LAYER : 6 * LAYER])
+        multiply(lefts[step], 6, high, 0, tmp.at[6 * LAYER : high * LAYER])
         own_apply(step, going)
         if going:
             inward = 0 if low % 2 else 3

time: 42.7 us -> 42.4 us (level)
  no operation moved by 1% of the time
where the time goes in v13:
time: 42.4 us; the launch traced here: 42 us
  Pallas kernels  41.2 us (97%)
  local copies, waits for them, and re-layouts  0.8 us (2%)
    pallas_call x1, Pallas kernels, per_device(): pl.pallas_call(kernel, out_shape=pltpu.VMEM(own, F32), in_specs=[hbm] * 8...  41.2 us

profile of v13, /device:TPU:7, one launch (start us, length us, event | category | flops | bytes accessed | tf_op | source)
XLA Modules:
  0.0 42.0 jit_solution(3680099307168531872)
XLA Ops:
  0.0 41.2 %solve_and_analyse.1 = f32[256,512]{1,0:T(8,128)S(1)} custom-call(f32[3,256,512]{2,1,0:T(8,128)} %forcing.1, f32[1,256]{1,0:T(1,128)} %bitcast.4, f32[1,256]{1,0:T(1,128)} %bitcast.5, s32[1,256]{1,0:T(1,128)} %order_in.1, s32[1,256]{1,0:T(1,128)} %owner_in.1, f32[8,512]{1,0:T(8,128)} %constant.6.clone.lanes_in, bf16[640,384]{1,0:T(8,128)(2,1)} %constant.7.clone.flat_in, ...), custom_call_target="tpu_custom_call" | custom-call | tf_op jit(solution)/shard_map/solve_and_analyse/pallas_call | solution.py:946
  41.2 0.8 %copy.10 = f32[1,256,512]{2,1,0:T(8,128)} copy(f32[1,256,512]{2,1,0:T(8,128)S(1)} %bitcast.3) | data formatting | bytes 1048576

commit v14 on v13

--- a/solution.py
+++ b/solution.py
@@ -510,7 +510,8 @@
     over(3, 9, first_faces)
     for layer in (2, 9):
         first_value(layer, 3, face_sum(tmp, layer, 3))
-    multiply(lhs0, 3, 9, 0, tmp.at[3 * LAYER : 9 * LAYER])
+    multiply(lhs0, 3, 6, 0, tmp.at[3 * LAYER : 6 * LAYER])
+    multiply(lhs0, 6, 9, 0, tmp.at[6 * LAYER : 9 * LAYER])
     own_apply(0, True)
     for layer in (3, 8):
         apply(0, layer, every, None, True)

time: 42.4 us -> 42.4 us (level)
  no operation moved by 1% of the time
where the time goes in v14:
time: 42.4 us; the launch traced here: 42 us
  Pallas kernels  41.2 us (97%)
  local copies, waits for them, and re-layouts  0.8 us (2%)
    pallas_call x1, Pallas kernels, per_device(): pl.pallas_call(kernel, out_shape=pltpu.VMEM(own, F32), in_specs=[hbm] * 8...  41.2 us

profile of v14, /device:TPU:7, one launch (start us, length us, event | category | flops | bytes accessed | tf_op | source)
XLA Modules:
  0.0 42.0 jit_solution(3772352930490375862)
XLA Ops:
  0.0 41.2 %solve_and_analyse.1 = f32[256,512]{1,0:T(8,128)S(1)} custom-call(f32[3,256,512]{2,1,0:T(8,128)} %forcing.1, f32[1,256]{1,0:T(1,128)} %bitcast.4, f32[1,256]{1,0:T(1,128)} %bitcast.5, s32[1,256]{1,0:T(1,128)} %order_in.1, s32[1,256]{1,0:T(1,128)} %owner_in.1, f32[8,512]{1,0:T(8,128)} %constant.6.clone.lanes_in, bf16[640,384]{1,0:T(8,128)(2,1)} %constant.7.clone.flat_in, ...), custom_call_target="tpu_custom_call" | custom-call | tf_op jit(solution)/shard_map/solve_and_analyse/pallas_call | solution.py:947
  41.2 0.8 %copy.10 = f32[1,256,512]{2,1,0:T(8,128)} copy(f32[1,256,512]{2,1,0:T(8,128)S(1)} %bitcast.3) | data formatting | bytes 1048576
